TPU v7x, 32 devices: a whole 2x2x4 slice. The times are simulated.
32 devices in a mesh: grp: 2 (over x), sp: 16 (over z, y, core).
Axes of the slice: x: 2, y: 2, z: 4, core: 2. Of those that a mesh axis runs over, the one named last changes fastest.
Arguments:
- latents: bfloat16 [10240, 64], P(('grp', 'sp')), parts along dimension 0, may hold values from -9 to 9
- row_cell: int32 [10240], P(('grp', 'sp')), parts along dimension 0, may hold values from 0 to 5119, as said below
- w_in: bfloat16 [3, 3, 3, 16, 384], replicated, may hold values from -1 to 1
- b_in: float32 [384], replicated, may hold values from -3 to 3
- gain: float32 [384], replicated, may hold values from 0.1 to 1.9
- w_mid: bfloat16 [3, 3, 3, 384, 384], replicated, may hold values from -0.0625 to 0.0625
- b_mid: float32 [384], replicated, may hold values from -3 to 3
Outputs:
- decoded: bfloat16 [32, 2, 4, 160, 384], P(('grp', 'sp')), parts along dimension 0
There are 2 independent parts, one for each index of `grp`. A program takes and returns all parts, laid end to end along the dimension named above; an argument that names none is the same for every part. Nothing has to cross between parts.
Inputs may be any that keep to these rules, and one draw needn't show every extreme that they name: `row_cell`: every token position appears exactly once. The tile of token (t, i, j) is (t // 2) * 8 + (2 i) // 4. Among the tokens of one device, every tile has 20 tokens, except one tile with 40 and one with none; each tile gets 2 * 20 tokens from exactly one device. Order within a device is arbitrary.
All inputs are finite; a program needn't handle non-finite values.
Results may differ from a plain program's by a relative error of at most 0.0051.
Values may be sent and summed in bfloat16 or wider, within the bound.
No kernel may reach another device: no remote copies, remote signals or barrier semaphores. Data moves between devices by JAX's collectives and lax.ppermute only.
A program may use at most 128 MiB of HBM per device.

v0:
```python
import jax
import jax.numpy as jnp
from jax import lax
from jax.sharding import PartitionSpec as P

C_LAT = 16
W = 160
TB = 2
HBANDS = 8
HB = 4
TOKS = 320


def passed_along(value, axis, steps):
    count = lax.axis_size(axis)
    pairs = [(source, (source + steps) % count) for source in range(count)]
    return lax.ppermute(value, axis, pairs)


def with_halo(block, sides, width):
    for axis, dim in sides:
        count = lax.axis_size(axis)
        forward = [(i, i + 1) for i in range(count - 1)]
        forward.append((count - 1, 0))
        backward = [(target, source) for source, target in forward]
        low = lax.ppermute(
            lax.slice_in_dim(block, block.shape[dim] - width, None, axis=dim), axis, forward
        )
        high = lax.ppermute(lax.slice_in_dim(block, 0, width, axis=dim), axis, backward)
        block = jnp.concatenate([low, block, high], axis=dim)
    return block


def causal_conv(extended, weight):
    frames_out = extended.shape[0] - 2
    rows_out = extended.shape[1] - 2
    tile_width = extended.shape[2]
    channels = extended.shape[3]
    outputs = weight.shape[4]
    padded = jnp.pad(extended, ((0, 0), (0, 0), (1, 1), (0, 0)))
    widened = jnp.concatenate(
        [padded[:, :, offset : offset + tile_width] for offset in range(3)], axis=3
    )
    accumulated = jnp.zeros((frames_out, rows_out, tile_width, outputs), jnp.float32)
    for tap_time in range(3):
        for tap_row in range(3):
            window = widened[tap_time : tap_time + frames_out, tap_row : tap_row + rows_out]
            kernel = weight[tap_time, tap_row].reshape(3 * channels, outputs)
            accumulated = accumulated + jnp.einsum(
                "thwc,cd->thwd", window, kernel, preferred_element_type=jnp.float32
            )
    return accumulated


def rms_silu(hidden, gain):
    values = hidden.astype(jnp.float32)
    inverse_rms = lax.rsqrt(jnp.mean(values * values, axis=-1, keepdims=True) + 1e-06)
    return jax.nn.silu(values * inverse_rms * gain).astype(jnp.bfloat16)


def band_mask(extended, band_index, margin):
    row_count = extended.shape[1]
    global_row = band_index * HB - margin + jnp.arange(row_count, dtype=jnp.int32)
    inside = (global_row >= 0) & (global_row < HB * HBANDS)
    return jnp.where(inside[None, :, None, None], extended, jnp.zeros((), extended.dtype))


def keep_when(flag, values):
    return jnp.where(flag, values, jnp.zeros((), values.dtype))


def margin_tail(rimmed, band_index, time_block, w_in, b_in, gain):
    hidden_wide = (causal_conv(rimmed, w_in) + b_in).astype(jnp.bfloat16)
    active_wide = band_mask(rms_silu(hidden_wide, gain), band_index, 1)
    frame_valid = time_block * TB - 2 + jnp.arange(TB + 2, dtype=jnp.int32) >= 0
    activated = jnp.where(
        frame_valid[:, None, None, None], active_wide, jnp.zeros((), active_wide.dtype)
    )
    return (activated, hidden_wide[2:, 1:-1])


def shards(latents, row_cell, w_in, b_in, gain, w_mid, b_mid):
    devices = lax.axis_size("sp")
    position = lax.axis_index("sp")
    offset_tiles = 2 * HBANDS + HBANDS // 2
    tile_index = (position + offset_tiles) % devices
    band_index = tile_index % HBANDS
    time_block = tile_index // HBANDS
    slot_count = 2 * (TOKS // devices)
    half_rows = HB // 2
    half_width = W // 2
    channels_in = latents.shape[1]
    column = row_cell % half_width
    token_row = row_cell // half_width % (half_rows * HBANDS)
    frame_index = row_cell // (half_width * half_rows * HBANDS)
    owner_tile = frame_index // TB * HBANDS + token_row // half_rows
    frame_within = frame_index % TB
    row_within = token_row % half_rows
    local_index = (frame_within * half_rows + row_within) * half_width + column
    owner_hits = (owner_tile[:, None] == jnp.arange(devices, dtype=jnp.int32)[None, :]).astype(
        jnp.int32
    )
    earlier = jnp.cumsum(owner_hits, axis=0) - owner_hits
    slot_rank = jnp.sum(earlier * owner_hits, axis=1)
    owner_device = (owner_tile - offset_tiles) % devices
    target = owner_device * slot_count + slot_rank
    outgoing = jnp.zeros((devices * slot_count, channels_in), latents.dtype).at[target].set(latents)
    places = jnp.full((devices * slot_count,), TOKS, jnp.int32).at[target].set(local_index)
    arrived, arrived_places = (
        lax.all_to_all(
            outgoing.reshape(devices, slot_count, channels_in),
            "sp",
            split_axis=0,
            concat_axis=0,
            tiled=True,
        ),
        lax.all_to_all(
            places.reshape(devices, slot_count), "sp", split_axis=0, concat_axis=0, tiled=True
        ),
    )
    flat_arrived = arrived.reshape(devices * slot_count, channels_in)
    flat_places = arrived_places.reshape(-1)
    tile_tokens = (
        jnp.zeros((TOKS, channels_in), latents.dtype).at[flat_places].set(flat_arrived, mode="drop")
    )
    latent_grid = tile_tokens.reshape(TB, half_rows, half_width, 2, 2, C_LAT)
    latent_grid = latent_grid.transpose(0, 1, 3, 2, 4, 5).reshape(TB, HB, W, C_LAT)
    prior_block = keep_when(time_block >= 1, passed_along(latent_grid, "sp", HBANDS))
    older_block = keep_when(time_block >= 2, passed_along(latent_grid, "sp", 2 * HBANDS))
    stacked = jnp.concatenate([older_block, prior_block, latent_grid], axis=0)
    rimmed = band_mask(with_halo(stacked, (("sp", 1),), 2), band_index, 2)
    activated, hidden = margin_tail(rimmed, band_index, time_block, w_in, b_in, gain)
    mixed = causal_conv(activated, w_mid) + b_mid + hidden.astype(jnp.float32)
    return mixed.astype(jnp.bfloat16)[None]


def solution(mesh):
    return jax.shard_map(
        shards,
        mesh=mesh,
        in_specs=(P(("grp", "sp"), None), P(("grp", "sp")), P(), P(), P(), P(), P()),
        out_specs=P(("grp", "sp"), None, None, None, None),
        check_vma=False,
    )
```

profile of v0, /device:TPU:0, one launch (start us, length us, event | category | flops | bytes accessed | tf_op | source)
XLA Modules:
  0.0 124.3 jit_solution(10751556660676795817)
XLA Ops:
  2.0 2.9 %scatter_custom_fusion = s32[640]{0:T(1024)S(1)} fusion(s32[320]{0:T(512)S(1)} %compare_select_fusion.1, s32[320]{0:T(512)S(1)} %get-tuple-element.29, s32[]{:T(128)} %constant.143.clone.1), kind=kCustom, calls=%fused_computation.79 | custom fusion | bytes 2564 | tf_op jit(solution)/shard_map/scatter | solution.py:108
  5.6 7.4 %all-to-all-start = ((s32[16,1,40]{2,1,0:T(1,128)}), s32[16,1,40]{2,1,0:T(1,128)S(1)}, u32[]{:S(2)}, u32[]{:S(2)}) async-start(s32[16,1,40]{2,1,0:T(1,128)} %all_to_all.9), calls=%async_computation | async-start | bytes 16384 | tf_op jit(solution)/shard_map/all_to_all | solution.py:117
  13.1 5.4 %fusion.41 = (bf16[1,1,3,384,384]{4,3,2,1,0:T(8,128)(2,1)}, bf16[1,1,3,384,384]{4,3,2,1,0:T(8,128)(2,1)}, bf16[1,1,3,384,384]{4,3,2,1,0:T(8,128)(2,1)}, bf16[1,1...) fusion(bf16[3,3,3,384,384]{4,3,2,1,0:T(8,128)(2,1)} %param.12), kind=kLoop, calls=%fused_computation.98 | loop fusion | bytes 15925248 | tf_op jit(solution)/shard_map/slice | solution.py:48
  20.8 6.0 %all-to-all-start.1 = ((bf16[16,2,1280]{2,1,0:T(2,128)(2,1)}), bf16[16,2,1280]{2,1,0:T(2,128)(2,1)S(1)}, u32[]{:S(2)}, u32[]{:S(2)}) async-start(bf16[16,2,1280]{2,1,0:T(2,128)(2,1)} %reshape.159), calls=%async_computation.1 | async-start | bytes 163840 | tf_op jit(solution)/shard_map/all_to_all | solution.py:110
  28.1 5.9 %all-to-all-done.1 = bf16[16,2,1280]{2,1,0:T(2,128)(2,1)S(1)} async-done(((bf16[16,2,1280]{2,1,0:T(2,128)(2,1)}), bf16[16,2,1280]{2,1,0:T(2,128)(2,1)S(1)}, u32[]{:S(2)}, u32[]{:S(2)}) %all-to-all-start.1) | async-done | bytes 81952 | tf_op jit(solution)/shard_map/all_to_all | solution.py:110
  34.1 4.2 %scatter_custom_fusion.2 = bf16[320,64]{1,0:T(8,128)(2,1)S(1)} fusion(s32[640]{0:T(1024)S(1)} %fusion.17, bf16[640,64]{1,0:T(8,128)(2,1)S(1)} %bitcast.153, bf16[]{:T(256)} %constant.142.clone.1), kind=kCustom, calls=%fused_computation.30 | custom fusion | bytes 40962 | tf_op jit(solution)/shard_map/scatter | solution.py:124
  39.2 5.6 %collective-permute-done.1 = bf16[2,4,160,16]{2,3,1,0:T(8,128)(2,1)S(1)} collective-permute-done((bf16[2,4,160,16]{2,3,1,0:T(8,128)(2,1)S(1)}, bf16[2,4,160,16]{2,3,1,0:T(8,128)(2,1)S(1)}, u32[]{:S(2)}, u32[]{:S(2)}) %collective-permute-start.1) | collective-permute-done | bytes 40992 | tf_op jit(solution)/shard_map/ppermute | solution.py:17
  45.0 4.4 %collective-permute-start.3 = (bf16[6,2,160,16]{2,3,1,0:T(8,128)(2,1)S(1)}, bf16[6,2,160,16]{2,3,1,0:T(8,128)(2,1)S(1)}, u32[]{:S(2)}, u32[]{:S(2)}) collective-permute-start(bf16[6,2,160,16]{2,3,1,0:T(8,128)(2,1)S(1)} %get-tuple-element.28), channel_id=1, source_target_pairs={{1,0},{2,1},{3,2},{4,3},{5,4},{6,5},{7,6},{8,7},{9,8},{10,9},{11,1... | collective-permute-start | bytes 184328 | tf_op jit(solution)/shard_map/ppermute | solution.py:29
  49.4 2.3 %collective-permute-done.2 = bf16[6,2,160,16]{2,3,1,0:T(8,128)(2,1)S(1)} collective-permute-done((bf16[6,2,160,16]{2,3,1,0:T(8,128)(2,1)S(1)}, bf16[6,2,160,16]{2,3,1,0:T(8,128)(2,1)S(1)}, u32[]{:S(2)}, u32[]{:S(2)}) %collective-permute-start.2) | collective-permute-done | bytes 61472 | tf_op jit(solution)/shard_map/ppermute | solution.py:26
  52.2 3.5 %fusion.39 = f32[4,6,160,384]{3,2,1,0:T(8,128)} fusion(bf16[48,384,1,1]{1,0,3,2:T(8,128)(2,1)S(1)} %bitcast.162, bf16[6,8,160,16]{2,3,1,0:T(8,128)(2,1)S(1)} %get-tuple-element.17, bf16[6,8,160,16]{2,3,1,0:T(8,128)(2,1)S(1)} %maximum_select_fusion, bf16[6,8,160,16]{2,3,1,0:T(8,128)(2,1)S(1)} %get-tuple-element.16), kind=kOutput, calls=%fused_computation.96 | convolution fusion | flops 143769600 | bytes 6672384 | tf_op jit(solution)/shard_map/thwc,cd->thwd/dot_general | solution.py:49
  55.7 3.5 %fusion.38 = f32[4,6,160,384]{3,2,1,0:T(8,128)} fusion(bf16[48,384,1,1]{1,0,3,2:T(8,128)(2,1)S(1)} %bitcast.161, bf16[6,8,160,16]{2,3,1,0:T(8,128)(2,1)S(1)} %get-tuple-element.17, bf16[6,8,160,16]{2,3,1,0:T(8,128)(2,1)S(1)} %maximum_select_fusion, bf16[6,8,160,16]{2,3,1,0:T(8,128)(2,1)S(1)} %get-tuple-element.16), kind=kOutput, calls=%fused_computation.95 | convolution fusion | flops 143769600 | bytes 6672384 | tf_op jit(solution)/shard_map/thwc,cd->thwd/dot_general | solution.py:49
  59.1 3.4 %fusion.37 = f32[4,6,160,384]{3,2,1,0:T(8,128)} fusion(bf16[48,384,1,1]{1,0,3,2:T(8,128)(2,1)S(1)} %bitcast.160, bf16[6,8,160,16]{2,3,1,0:T(8,128)(2,1)S(1)} %get-tuple-element.17, bf16[6,8,160,16]{2,3,1,0:T(8,128)(2,1)S(1)} %maximum_select_fusion, bf16[6,8,160,16]{2,3,1,0:T(8,128)(2,1)S(1)} %get-tuple-element.16), kind=kOutput, calls=%fused_computation.94 | convolution fusion | flops 143769600 | bytes 6672384 | tf_op jit(solution)/shard_map/thwc,cd->thwd/dot_general | solution.py:49
  62.6 3.5 %fusion.36 = f32[4,6,160,384]{3,2,1,0:T(8,128)} fusion(bf16[48,384,1,1]{1,0,3,2:T(8,128)(2,1)S(1)} %bitcast.159, bf16[6,8,160,16]{2,3,1,0:T(8,128)(2,1)S(1)} %get-tuple-element.17, bf16[6,8,160,16]{2,3,1,0:T(8,128)(2,1)S(1)} %maximum_select_fusion, bf16[6,8,160,16]{2,3,1,0:T(8,128)(2,1)S(1)} %get-tuple-element.16), kind=kOutput, calls=%fused_computation.93 | convolution fusion | flops 143769600 | bytes 6672384 | tf_op jit(solution)/shard_map/thwc,cd->thwd/dot_general | solution.py:49
  66.1 3.5 %fusion.35 = f32[4,6,160,384]{3,2,1,0:T(8,128)} fusion(bf16[48,384,1,1]{1,0,3,2:T(8,128)(2,1)S(1)} %bitcast.158, bf16[6,8,160,16]{2,3,1,0:T(8,128)(2,1)S(1)} %get-tuple-element.17, bf16[6,8,160,16]{2,3,1,0:T(8,128)(2,1)S(1)} %maximum_select_fusion, bf16[6,8,160,16]{2,3,1,0:T(8,128)(2,1)S(1)} %get-tuple-element.16), kind=kOutput, calls=%fused_computation.92 | convolution fusion | flops 143769600 | bytes 6672384 | tf_op jit(solution)/shard_map/thwc,cd->thwd/dot_general | solution.py:49
  69.6 3.6 %fusion.34 = f32[4,6,160,384]{3,2,1,0:T(8,128)} fusion(bf16[48,384,1,1]{1,0,3,2:T(8,128)(2,1)S(1)} %bitcast.157, bf16[6,8,160,16]{2,3,1,0:T(8,128)(2,1)S(1)} %get-tuple-element.17, bf16[6,8,160,16]{2,3,1,0:T(8,128)(2,1)S(1)} %maximum_select_fusion, bf16[6,8,160,16]{2,3,1,0:T(8,128)(2,1)S(1)} %get-tuple-element.16), kind=kOutput, calls=%fused_computation.91 | convolution fusion | flops 143769600 | bytes 6672384 | tf_op jit(solution)/shard_map/thwc,cd->thwd/dot_general | solution.py:49
  73.1 3.5 %fusion.33 = f32[4,6,160,384]{3,2,1,0:T(8,128)} fusion(bf16[48,384,1,1]{1,0,3,2:T(8,128)(2,1)S(1)} %bitcast.156, bf16[6,8,160,16]{2,3,1,0:T(8,128)(2,1)S(1)} %get-tuple-element.17, bf16[6,8,160,16]{2,3,1,0:T(8,128)(2,1)S(1)} %maximum_select_fusion, bf16[6,8,160,16]{2,3,1,0:T(8,128)(2,1)S(1)} %get-tuple-element.16), kind=kOutput, calls=%fused_computation.90 | convolution fusion | flops 143769600 | bytes 6672384 | tf_op jit(solution)/shard_map/thwc,cd->thwd/dot_general | solution.py:49
  76.6 3.5 %fusion.40 = f32[4,6,160,384]{3,2,1,0:T(8,128)} fusion(bf16[48,384,1,1]{1,0,3,2:T(8,128)(2,1)S(1)} %bitcast.155, bf16[6,8,160,16]{2,3,1,0:T(8,128)(2,1)S(1)} %get-tuple-element.17, bf16[6,8,160,16]{2,3,1,0:T(8,128)(2,1)S(1)} %maximum_select_fusion, bf16[6,8,160,16]{2,3,1,0:T(8,128)(2,1)S(1)} %get-tuple-element.16), kind=kOutput, calls=%fused_computation.97 | convolution fusion | flops 143769600 | bytes 6672384 | tf_op jit(solution)/shard_map/thwc,cd->thwd/dot_general | solution.py:49
  80.1 17.7 %fusion = (f32[4,6,160]{2,1,0:T(8,128)S(1)}, bf16[4,6,160,384]{3,2,1,0:T(8,128)(2,1)}) fusion(f32[384]{0:T(512)S(1)} %copy-done.11, bf16[48,384,1,1]{1,0,3,2:T(8,128)(2,1)S(1)} %bitcast.154, bf16[6,8,160,16]{2,3,1,0:T(8,128)(2,1)S(1)} %get-tuple-element.17, bf16[6,8,160,16]{2,3,1,0:T(8,128)(2,1)S(1)} %maximum_select_fusion, ...), kind=kOutput, calls=%fused_computation.6 | convolution fusion | flops 162935040 | bytes 50926080 | tf_op jit(solution)/shard_map/thwc,cd->thwd/dot_general | solution.py:49
  97.8 3.6 %fusion.9 = bf16[4,6,160,384]{3,2,1,0:T(8,128)(2,1)S(1)} fusion(bf16[4,6,160,384]{3,2,1,0:T(8,128)(2,1)} %get-tuple-element.32, f32[384]{0:T(512)S(1)} %copy-done.10, f32[4,6,160]{2,1,0:T(8,128)S(1)} %add_rsqrt_fusion, pred[6]{0:T(512)(128)(4,1)S(1)} %compare_and_fusion.1, pred[4]{0:T(512)(128)(4,1)S(1)} %add_compare_fusion), kind=kLoop, calls=%fused_computation.16 | loop fusion | flops 14745600 | bytes 5915146 | tf_op jit(solution)/shard_map/jit(_where)/select_n | solution.py:76
  101.4 2.5 %pad_slice_fusion.1 = (bf16[4,6,160,384]{3,2,1,0:T(8,128)(2,1)S(1)}, bf16[4,6,160,384]{3,2,1,0:T(8,128)(2,1)S(1)}) fusion(bf16[4,6,160,384]{3,2,1,0:T(8,128)(2,1)S(1)} %fusion.9), kind=kLoop, calls=%fused_computation.18 | loop fusion | bytes 8847360 | tf_op jit(solution)/shard_map/slice | solution.py:42
  105.1 1.8 %fusion.50 = f32[2,4,160,384]{3,2,1,0:T(8,128)S(1)} fusion(bf16[4,6,160,1152]{3,2,1,0:T(8,128)(2,1)S(1)} %pad_maximum_fusion, bf16[1152,384,1,1]{1,0,3,2:T(8,128)(2,1)S(1)} %bitcast.150), kind=kOutput, calls=%fused_computation.107 | convolution fusion | flops 1132462080 | bytes 11698176 | tf_op jit(solution)/shard_map/thwc,cd->thwd/dot_general | solution.py:49
  106.9 1.8 %fusion.45 = f32[2,4,160,384]{3,2,1,0:T(8,128)S(1)} fusion(bf16[4,6,160,1152]{3,2,1,0:T(8,128)(2,1)S(1)} %pad_maximum_fusion, bf16[1152,384,1,1]{1,0,3,2:T(8,128)(2,1)S(1)} %bitcast.149), kind=kOutput, calls=%fused_computation.102 | convolution fusion | flops 1132462080 | bytes 11698176 | tf_op jit(solution)/shard_map/thwc,cd->thwd/dot_general | solution.py:49
  117.7 1.8 %fusion.51 = f32[2,4,160,384]{3,2,1,0:T(8,128)S(1)} fusion(bf16[4,6,160,1152]{3,2,1,0:T(8,128)(2,1)S(1)} %pad_maximum_fusion, bf16[1152,384,1,1]{1,0,3,2:T(8,128)(2,1)S(1)} %bitcast.143), kind=kOutput, calls=%fused_computation.108 | convolution fusion | flops 1132462080 | bytes 11698176 | tf_op jit(solution)/shard_map/thwc,cd->thwd/dot_general | solution.py:49
  119.5 4.8 %fusion.10 = bf16[1,2,4,160,384]{4,3,2,1,0:T(8,128)(2,1)} fusion(bf16[4,6,160,1152]{3,2,1,0:T(8,128)(2,1)S(1)} %pad_maximum_fusion, bf16[1152,384,1,1]{1,0,3,2:T(8,128)(2,1)S(1)} %bitcast.141, f32[2,4,160,384]{3,2,1,0:T(8,128)S(1)} %fusion.51, f32[2,4,160,384]{3,2,1,0:T(8,128)S(1)} %fusion.50, f32[2,4,160,384]{3,2,1,0:T(8,128)S(1)} %fusion.49, ...), kind=kOutput, calls=%fused_computation.20 | convolution fusion | flops 1138360320 | bytes 27428352 | tf_op jit(solution)/shard_map/thwc,cd->thwd/dot_general | solution.py:49
  (69 shorter events, 17.8 us)
Async XLA Ops:
  5.6 15.2 %all-to-all-start = ((s32[16,1,40]{2,1,0:T(1,128)}), s32[16,1,40]{2,1,0:T(1,128)S(1)}, u32[]{:S(2)}, u32[]{:S(2)}) async-start(s32[16,1,40]{2,1,0:T(1,128)} %all_to_all.9), calls=%async_computation | async-start | bytes 16384 | tf_op jit(solution)/shard_map/all_to_all | solution.py:117
  13.0 5.4 %copy-start.7 = (bf16[3,3,3,16,384]{4,3,2,1,0:T(8,128)(2,1)S(1)}, bf16[3,3,3,16,384]{4,3,2,1,0:T(8,128)(2,1)}, u32[]{:S(2)}) copy-start(bf16[3,3,3,16,384]{4,3,2,1,0:T(8,128)(2,1)} %param.9) | copy-start | bytes 995332
  13.1 5.5 %copy-start.8 = (bf16[320,64]{0,1:T(8,128)(2,1)S(1)}, bf16[320,64]{0,1:T(8,128)(2,1)}, u32[]{:S(2)}) copy-start(bf16[320,64]{0,1:T(8,128)(2,1)} %param.7) | copy-start | bytes 122884
  20.8 13.1 %all-to-all-start.1 = ((bf16[16,2,1280]{2,1,0:T(2,128)(2,1)}), bf16[16,2,1280]{2,1,0:T(2,128)(2,1)S(1)}, u32[]{:S(2)}, u32[]{:S(2)}) async-start(bf16[16,2,1280]{2,1,0:T(2,128)(2,1)} %reshape.159), calls=%async_computation.1 | async-start | bytes 163840 | tf_op jit(solution)/shard_map/all_to_all | solution.py:110
  39.0 5.8 %collective-permute-start.1 = (bf16[2,4,160,16]{2,3,1,0:T(8,128)(2,1)S(1)}, bf16[2,4,160,16]{2,3,1,0:T(8,128)(2,1)S(1)}, u32[]{:S(2)}, u32[]{:S(2)}) collective-permute-start(bf16[2,4,160,16]{2,3,1,0:T(8,128)(2,1)S(1)} %copy.21), channel_id=1, source_target_pairs={{0,8},{1,9},{2,10},{3,11},{4,12},{5,13},{6,14},{7,15},{8,0},{9,1},... | collective-permute-start | bytes 122888 | tf_op jit(solution)/shard_map/ppermute | solution.py:17
  39.2 5.6 %collective-permute-start = (bf16[2,4,160,16]{2,3,1,0:T(8,128)(2,1)S(1)}, bf16[2,4,160,16]{2,3,1,0:T(8,128)(2,1)S(1)}, u32[]{:S(2)}, u32[]{:S(2)}) collective-permute-start(bf16[2,4,160,16]{2,3,1,0:T(8,128)(2,1)S(1)} %copy.21), channel_id=1, source_target_pairs={{0,0},{1,1},{2,2},{3,3},{4,4},{5,5},{6,6},{7,7},{8,8},{9,9},{10,10... | collective-permute-start | bytes 122888 | tf_op jit(solution)/shard_map/ppermute | solution.py:17
  44.9 6.8 %collective-permute-start.2 = (bf16[6,2,160,16]{2,3,1,0:T(8,128)(2,1)S(1)}, bf16[6,2,160,16]{2,3,1,0:T(8,128)(2,1)S(1)}, u32[]{:S(2)}, u32[]{:S(2)}) collective-permute-start(bf16[6,2,160,16]{2,3,1,0:T(8,128)(2,1)S(1)} %get-tuple-element.27), channel_id=1, source_target_pairs={{0,1},{1,2},{2,3},{3,4},{4,5},{5,6},{6,7},{7,8},{8,9},{9,10},{10,1... | collective-permute-start | bytes 184328 | tf_op jit(solution)/shard_map/ppermute | solution.py:26
  45.0 6.7 %collective-permute-start.3 = (bf16[6,2,160,16]{2,3,1,0:T(8,128)(2,1)S(1)}, bf16[6,2,160,16]{2,3,1,0:T(8,128)(2,1)S(1)}, u32[]{:S(2)}, u32[]{:S(2)}) collective-permute-start(bf16[6,2,160,16]{2,3,1,0:T(8,128)(2,1)S(1)} %get-tuple-element.28), channel_id=1, source_target_pairs={{1,0},{2,1},{3,2},{4,3},{5,4},{6,5},{7,6},{8,7},{9,8},{10,9},{11,1... | collective-permute-start | bytes 184328 | tf_op jit(solution)/shard_map/ppermute | solution.py:29
  76.6 3.5 %copy-start.11 = (f32[384]{0:T(512)S(1)}, f32[384]{0:T(512)}, u32[]{:S(2)}) copy-start(f32[384]{0:T(512)} %param.10) | copy-start | bytes 4612
  80.1 17.7 %copy-start.10 = (f32[384]{0:T(512)S(1)}, f32[384]{0:T(512)}, u32[]{:S(2)}) copy-start(f32[384]{0:T(512)} %param.11) | copy-start | bytes 4612
  103.9 1.2 copy-start.6
  105.1 1.8 %copy-start.5 = (bf16[1,1,3,384,384]{4,3,2,1,0:T(8,128)(2,1)S(1)}, bf16[1,1,3,384,384]{4,3,2,1,0:T(8,128)(2,1)}, u32[]{:S(2)}) copy-start(bf16[1,1,3,384,384]{4,3,2,1,0:T(8,128)(2,1)} %get-tuple-element.5) | copy-start | bytes 2654212
  106.9 1.8 %copy-start.4 = (bf16[1,1,3,384,384]{4,3,2,1,0:T(8,128)(2,1)S(1)}, bf16[1,1,3,384,384]{4,3,2,1,0:T(8,128)(2,1)}, u32[]{:S(2)}) copy-start(bf16[1,1,3,384,384]{4,3,2,1,0:T(8,128)(2,1)} %get-tuple-element.7) | copy-start | bytes 2654212
  108.7 1.8 %copy-start.3 = (bf16[1,1,3,384,384]{4,3,2,1,0:T(8,128)(2,1)S(1)}, bf16[1,1,3,384,384]{4,3,2,1,0:T(8,128)(2,1)}, u32[]{:S(2)}) copy-start(bf16[1,1,3,384,384]{4,3,2,1,0:T(8,128)(2,1)} %get-tuple-element.8) | copy-start | bytes 2654212
  110.5 1.8 %copy-start.2 = (bf16[1,1,3,384,384]{4,3,2,1,0:T(8,128)(2,1)S(1)}, bf16[1,1,3,384,384]{4,3,2,1,0:T(8,128)(2,1)}, u32[]{:S(2)}) copy-start(bf16[1,1,3,384,384]{4,3,2,1,0:T(8,128)(2,1)} %get-tuple-element.9) | copy-start | bytes 2654212
  112.3 1.8 %copy-start.1 = (bf16[1,1,3,384,384]{4,3,2,1,0:T(8,128)(2,1)S(1)}, bf16[1,1,3,384,384]{4,3,2,1,0:T(8,128)(2,1)}, u32[]{:S(2)}) copy-start(bf16[1,1,3,384,384]{4,3,2,1,0:T(8,128)(2,1)} %get-tuple-element.10) | copy-start | bytes 2654212
  114.1 1.8 %copy-start = (bf16[1,1,3,384,384]{4,3,2,1,0:T(8,128)(2,1)S(1)}, bf16[1,1,3,384,384]{4,3,2,1,0:T(8,128)(2,1)}, u32[]{:S(2)}) copy-start(bf16[1,1,3,384,384]{4,3,2,1,0:T(8,128)(2,1)} %get-tuple-element.11) | copy-start | bytes 2654212
  117.7 1.8 %copy-start.9 = (f32[384]{0:T(512)S(1)}, f32[384]{0:T(512)}, u32[]{:S(2)}) copy-start(f32[384]{0:T(512)} %param.13) | copy-start | bytes 4612
where the time goes:
time: 125 us; the launch traced here: 124 us
  matrix products  64.6 us (52%)
  local copies, waits for them, and re-layouts  20 us (16%)
  starting transfers between devices  18.1 us (14%)
  waiting for transfers between devices  13.8 us (11%)
  other arithmetic  7.33 us (6%)
    dot_general x18, matrix products, causal_conv(): jnp.einsum('thwc,cd->thwd', window, kernel, preferred_element_type=jnp.fl...  64.6 us
    all_to_all x1, starting transfers between devices, shards(): lax.all_to_all(places.reshape(devices, slot_count), 'sp', split_axis=0, c...  7.41 us
    all_to_all x1, starting transfers between devices, shards(): lax.all_to_all(outgoing.reshape(devices, slot_count, channels_in), 'sp',...  6.01 us
    all_to_all x1, waiting for transfers between devices, shards(): lax.all_to_all(outgoing.reshape(devices, slot_count, channels_in), 'sp',...  5.88 us
    ppermute x2, waiting for transfers between devices, passed_along(): return lax.ppermute(value, axis, pairs)  5.62 us
    slice x2, local copies, waits for them, and re-layouts, causal_conv(): kernel = weight[tap_time, tap_row].reshape(3 * channels, outputs)  5.44 us
    ppermute x1, starting transfers between devices, with_halo(): lax.ppermute(lax.slice_in_dim(block, 0, width, axis=dim), axis, backward)  4.43 us
    scatter x2, local copies, waits for them, and re-layouts, shards(): jnp.zeros((TOKS, channels_in), latents.dtype).at[flat_places]  4.32 us
  transfers between devices with their start and end apart: 6, of which 3 were waited for; matrix products, arithmetic and copies ran while one was open for 7% of the time, Pallas kernels for 0%

commit v1 on v0

v1 whole, which is shorter than its diff:
```python
import functools

import jax
import jax.numpy as jnp
from jax import lax
from jax.experimental import pallas as pl
from jax.experimental.pallas import tpu as pltpu
from jax.sharding import PartitionSpec as P

C_LAT = 16
W = 160
TB = 2
HBANDS = 8
HB = 4
OFFSET = 2 * HBANDS + HBANDS // 2
HALF_ROWS = HB // 2
HALF_W = W // 2
TILE_TOKENS = TB * HALF_ROWS * HALF_W
PATCH = 4 * C_LAT
F32 = jnp.float32
BF16 = jnp.bfloat16
VMEM = pl.BlockSpec(memory_space=pltpu.VMEM)
ANY = pl.BlockSpec(memory_space=pl.ANY)


def place_code(index):
    return ((index & 127) + 128) << (index >> 7)


def pack_kernel(devices, rows, half, cells_ref, latents_ref, out_ref):
    tokens = latents_ref.shape[0]
    cells = cells_ref[...]
    column = lax.rem(cells, HALF_W)
    token_row = lax.rem(lax.div(cells, HALF_W), HALF_ROWS * HBANDS)
    frame = lax.div(cells, HALF_W * HALF_ROWS * HBANDS)
    block = lax.div(frame, TB)
    band = lax.div(token_row, HALF_ROWS)
    side = lax.rem(token_row, HALF_ROWS)
    local = (lax.rem(frame, TB) * HALF_ROWS + side) * HALF_W + column
    code = place_code((lax.rem(block, 3) * 3 + lax.rem(band, 3)) * TILE_TOKENS + local)
    code = code.astype(F32)

    device = lax.broadcasted_iota(jnp.int32, (devices, tokens), 0)
    tile = lax.rem(device + OFFSET, devices)
    to_band = lax.rem(tile, HBANDS)
    age = lax.div(tile, HBANDS) - block
    near = (
        (band == to_band)
        | ((band == to_band - 1) & (side == HALF_ROWS - 1))
        | ((band == to_band + 1) & (side == 0))
    )
    hits = jnp.where((age >= 0) & (age < 3) & near, 1.0, 0.0)
    before = lax.broadcasted_iota(jnp.int32, (tokens, tokens), 0) < lax.broadcasted_iota(
        jnp.int32, (tokens, tokens), 1
    )
    before = jnp.where(before, 1.0, 0.0).astype(BF16)
    rank = jnp.dot(hits.astype(BF16), before, preferred_element_type=F32)
    rank = jnp.where(hits > 0.5, rank, -1.0)

    slot = lax.broadcasted_iota(jnp.int32, (rows, tokens), 0).astype(F32)
    low_slot = jnp.where(slot < half, slot, -7.0)
    high_slot = jnp.where(slot < half, slot + half, -7.0)
    low = jnp.concatenate(
        [jnp.where(rank[d : d + 1] == low_slot, 1.0, 0.0).astype(BF16) for d in range(devices)], 0
    )
    high = jnp.concatenate(
        [jnp.where(rank[d : d + 1] == high_slot, 1.0, 0.0).astype(BF16) for d in range(devices)], 0
    )
    latents = latents_ref[...]
    blank = jnp.zeros_like(latents)
    codes = jnp.transpose(jnp.broadcast_to(code, (128, tokens))).astype(BF16)
    low_out = jnp.dot(
        low, jnp.concatenate([latents, blank, codes], 1), preferred_element_type=F32
    )
    high_out = jnp.dot(
        high, jnp.concatenate([blank, latents, codes], 1), preferred_element_type=F32
    )
    row = lax.broadcasted_iota(jnp.int32, (rows, 128), 0)
    diagonal = row == lax.broadcasted_iota(jnp.int32, (rows, 128), 1)
    for d in range(devices):
        part = slice(d * rows, (d + 1) * rows)
        low_codes = jnp.sum(jnp.where(diagonal, low_out[part, 128:], 0.0), 0, keepdims=True)
        high_codes = jnp.sum(jnp.where(diagonal, high_out[part, 128:], 0.0), 0, keepdims=True)
        body = low_out[part, :128] + high_out[part, :128]
        body = jnp.where(row == rows - 2, low_codes, body)
        body = jnp.where(row == rows - 1, high_codes, body)
        out_ref[part, :] = body.astype(BF16)


def main_kernel(
    devices,
    blocks,
    arrived_ref,
    w_in_ref,
    b_in_ref,
    gain_ref,
    w_mid_hbm,
    b_mid_ref,
    out_ref,
    w_mid_ref,
    edge_ref,
    active_ref,
    hidden_ref,
    mix_ref,
    w_sem,
):
    weights_copy = pltpu.make_async_copy(w_mid_hbm, w_mid_ref, w_sem)
    weights_copy.start()
    total = arrived_ref.shape[0]
    rows = total // devices
    c_mid = gain_ref.shape[1]
    tile = lax.rem(lax.axis_index("sp") + OFFSET, devices)
    band = lax.rem(tile, HBANDS)
    time_block = lax.div(tile, HBANDS)

    arrived = arrived_ref[...]
    low_codes = jnp.concatenate(
        [arrived[(s + 1) * rows - 2 : (s + 1) * rows - 1, :rows] for s in range(devices)], 1
    ).astype(F32)
    high_codes = jnp.concatenate(
        [arrived[(s + 1) * rows - 1 : (s + 1) * rows, :rows] for s in range(devices)], 1
    ).astype(F32)
    k = lax.broadcasted_iota(jnp.int32, (128, 256), 0)
    lane = lax.broadcasted_iota(jnp.int32, (128, 256), 1)
    within = lane & 63
    swap = ((lane >> 6) ^ (lane >> 7)) & 1
    source = swap * (2 * C_LAT) + jnp.where(
        within < C_LAT,
        within + C_LAT,
        jnp.where(within < 3 * C_LAT, within - C_LAT, within - 3 * C_LAT),
    )
    low_spread = jnp.where(k == source, 1.0, 0.0).astype(BF16)
    high_spread = jnp.where(k == source + PATCH, 1.0, 0.0).astype(BF16)
    low_tokens = jnp.dot(arrived, low_spread, preferred_element_type=F32).astype(BF16)
    high_tokens = jnp.dot(arrived, high_spread, preferred_element_type=F32).astype(BF16)

    column = lax.broadcasted_iota(jnp.int32, (HALF_W, 1), 0)
    lanes = lax.broadcasted_iota(jnp.int32, (1, 1, 256), 2) & 63
    from_left, from_right = lanes < C_LAT, lanes >= 3 * C_LAT
    first = lax.broadcasted_iota(jnp.int32, (1, 1, 128), 2) < PATCH
    token_rows = HALF_ROWS + 2
    for f in range(TB * blocks):
        low_pick, high_pick = [], []
        frame = (time_block - (blocks - 1)) * TB + f
        for i in range(token_rows):
            token_row = band * HALF_ROWS - 1 + i
            valid = (frame >= 0) & (token_row >= 0) & (token_row < HALF_ROWS * HBANDS)
            frame_in = lax.max(frame, 0)
            row_in = lax.max(token_row, 0)
            base = (
                lax.rem(lax.div(frame_in, TB), 3) * 3 + lax.rem(lax.div(row_in, HALF_ROWS), 3)
            ) * TILE_TOKENS + (
                lax.rem(frame_in, TB) * HALF_ROWS + lax.rem(row_in, HALF_ROWS)
            ) * HALF_W
            code = jnp.where(valid, place_code(base + column), -1).astype(F32)
            low_pick.append(jnp.where(low_codes == code, 1.0, 0.0).astype(BF16))
            high_pick.append(jnp.where(high_codes == code, 1.0, 0.0).astype(BF16))
        placed = jnp.dot(
            jnp.concatenate(low_pick, 0), low_tokens, preferred_element_type=F32
        ) + jnp.dot(jnp.concatenate(high_pick, 0), high_tokens, preferred_element_type=F32)
        placed = placed.reshape(token_rows, HALF_W, 256)
        gap = jnp.zeros((token_rows, 1, 256), F32)
        left = jnp.concatenate([gap, placed[:, :-1]], 1)
        right = jnp.concatenate([placed[:, 1:], gap], 1)
        placed = jnp.where(from_left, left, jnp.where(from_right, right, placed))
        even_rows, odd_rows = placed[:, :, :128], placed[:, :, 128:]
        below = jnp.concatenate([odd_rows[1:], jnp.zeros((1, HALF_W, 128), F32)], 0)
        odd_rows = jnp.where(first, odd_rows, below)
        for i in range(token_rows):
            start = 2 * i * HALF_W
            edge_ref[f, start : start + HALF_W, :] = even_rows[i].astype(BF16)
            edge_ref[f, start + HALF_W : start + 2 * HALF_W, :] = odd_rows[i].astype(BF16)

    wide = (HB + 2) * HALF_W
    index = lax.broadcasted_iota(jnp.int32, (wide, 1), 0)
    global_row = band * HB - 1 + lax.div(index, HALF_W)
    inside = (global_row >= 0) & (global_row < HB * HBANDS)
    bias = b_in_ref[...]
    gain = gain_ref[...]
    for a in range(TB + 2):
        windows, kernels = [], []
        for tap in range(3):
            f = TB * (blocks - 1) - 4 + a + tap
            if f < 0:
                continue
            windows += [
                edge_ref[f, 0:wide, :],
                edge_ref[f, 2 * HALF_W : 2 * HALF_W + wide, :],
            ]
            kernels.append(w_in_ref[tap])
        sums = jnp.dot(
            jnp.concatenate(windows, 1), jnp.concatenate(kernels, 0), preferred_element_type=F32
        )
        keep = inside & (time_block * TB - 2 + a >= 0)
        for p in range(2):
            part = slice(p * c_mid, (p + 1) * c_mid)
            hidden = (sums[:, part] + bias).astype(BF16)
            if a >= 2:
                hidden_ref[a - 2, :, part] = hidden[HALF_W : HALF_W + HB * HALF_W]
            values = hidden.astype(F32)
            mean = jnp.sum(values * values, 1, keepdims=True) * (1.0 / c_mid)
            inverse = jnp.where(keep, lax.rsqrt(mean + 1e-06), 0.0)
            scaled = values * inverse * gain
            halved = scaled * 0.5
            active_ref[a, :, part] = (halved + halved * jnp.tanh(halved)).astype(BF16)

    weights_copy.wait()
    tall = HB * HALF_W
    for o in range(TB):
        windows, kernels = [], []
        evens, odds, rights, lefts = [], [], [], []
        for tap_time in range(3):
            for tap_row in range(3):
                start = tap_row * HALF_W
                windows.append(active_ref[o + tap_time, start : start + tall, :])
                w0, w1, w2 = (w_mid_ref[tap_time, tap_row, t] for t in range(3))
                kernels.append(jnp.concatenate([w1, w0], 1))
                kernels.append(jnp.concatenate([w2, w1], 1))
                evens.append(active_ref[o + tap_time, start : start + tall, :c_mid])
                odds.append(active_ref[o + tap_time, start : start + tall, c_mid:])
                rights.append(w2)
                lefts.append(w0)
        sums = jnp.dot(
            jnp.concatenate(windows, 1), jnp.concatenate(kernels, 0), preferred_element_type=F32
        )
        from_even = jnp.dot(
            jnp.concatenate(evens, 1), jnp.concatenate(rights, 0), preferred_element_type=F32
        ).reshape(HB, HALF_W, c_mid)
        from_odd = jnp.dot(
            jnp.concatenate(odds, 1), jnp.concatenate(lefts, 0), preferred_element_type=F32
        ).reshape(HB, HALF_W, c_mid)
        gap = jnp.zeros((HB, 1, c_mid), F32)
        to_odd = jnp.concatenate([from_even[:, 1:], gap], 1).reshape(tall, c_mid)
        to_even = jnp.concatenate([gap, from_odd[:, :-1]], 1).reshape(tall, c_mid)
        hidden = hidden_ref[o].astype(F32)
        bias_mid = b_mid_ref[...]
        even_out = sums[:, :c_mid] + to_even + bias_mid + hidden[:, :c_mid]
        odd_out = sums[:, c_mid:] + to_odd + bias_mid + hidden[:, c_mid:]
        for g in range(c_mid // 128):
            part = slice(g * 128, (g + 1) * 128)
            mix_ref[g, pl.ds(0, tall, stride=2), :] = even_out[:, part]
            mix_ref[g, pl.ds(1, tall, stride=2), :] = odd_out[:, part]
            out_ref[o * 2 * tall : (o + 1) * 2 * tall, part] = mix_ref[g].astype(BF16)


def input_kernel(w_in):
    c_mid = w_in.shape[-1]
    gap = jnp.zeros((3, 3, 1) + w_in.shape[3:], w_in.dtype)
    even = jnp.concatenate([w_in, gap], 2)
    odd = jnp.concatenate([gap, w_in], 2)
    both = jnp.concatenate([even, odd], -1).reshape(3, 3 * PATCH, 2 * c_mid)
    return jnp.pad(both, ((0, 0), (0, PATCH), (0, 0)))


def shards(latents, row_cell, w_in, b_in, gain, w_mid, b_mid):
    devices = lax.axis_size("sp")
    tokens = latents.shape[0]
    c_mid = gain.shape[0]
    blocks = min(3, devices // HBANDS)
    pair = tokens // devices
    slots = pair * 3 * blocks + pair
    half = -(-slots // 2)
    rows = -(-(half + 2) // 8) * 8
    outgoing = pl.pallas_call(
        functools.partial(pack_kernel, devices, rows, half),
        out_shape=jax.ShapeDtypeStruct((devices * rows, 128), BF16),
        in_specs=[VMEM, VMEM],
        out_specs=VMEM,
        name="pack",
    )(row_cell.reshape(1, tokens), latents)
    arrived = lax.all_to_all(
        outgoing.reshape(devices, rows, 128), "sp", split_axis=0, concat_axis=0, tiled=True
    )
    decoded = pl.pallas_call(
        functools.partial(main_kernel, devices, blocks),
        out_shape=jax.ShapeDtypeStruct((TB * HB * W, c_mid), BF16),
        in_specs=[VMEM, VMEM, VMEM, VMEM, ANY, VMEM],
        out_specs=VMEM,
        scratch_shapes=[
            pltpu.VMEM(w_mid.shape, BF16),
            pltpu.VMEM((TB * blocks, 2 * (HALF_ROWS + 2) * HALF_W, 128), BF16),
            pltpu.VMEM((TB + 2, (HB + 2) * HALF_W, 2 * c_mid), BF16),
            pltpu.VMEM((TB, HB * HALF_W, 2 * c_mid), BF16),
            pltpu.VMEM((c_mid // 128, HB * W, 128), F32),
            pltpu.SemaphoreType.DMA,
        ],
        compiler_params=pltpu.CompilerParams(vmem_limit_bytes=56 * 1024 * 1024),
        name="block",
    )(
        arrived.reshape(devices * rows, 128),
        input_kernel(w_in),
        b_in.reshape(1, c_mid),
        gain.reshape(1, c_mid),
        w_mid,
        b_mid.reshape(1, c_mid),
    )
    return decoded.reshape(1, TB, HB, W, c_mid)


def solution(mesh):
    return jax.shard_map(
        shards,
        mesh=mesh,
        in_specs=(P(("grp", "sp"), None), P(("grp", "sp")), P(), P(), P(), P(), P()),
        out_specs=P(("grp", "sp"), None, None, None, None),
        check_vma=False,
    )
```

time: 125 us -> 44.1 us (0.35)
  matrix products: 64.6 us -> 0 us
  Pallas kernels: 0 us -> 22.2 us
  local copies, waits for them, and re-layouts: 20 us -> 8.35 us
  starting transfers between devices: 18.1 us -> 7.41 us
  waiting for transfers between devices: 13.8 us -> 4.5 us
  other arithmetic: 7.33 us -> 1.21 us
    dot_general x18 -> x0, matrix products: 64.6 us -> none  [causal_conv(): jnp.einsum('thwc,cd->thwd', window, kernel, preferred_element_type=jnp.fl...]
    pallas_call x0 -> x2, Pallas kernels: none -> 22.2 us  [the longest x1 19.7 us: shards(): pl.pallas_call(functools.partial(main_kernel, devices, blocks), out_shape...]
    scatter x4 -> x0, local copies, waits for them, and re-layouts: 8.61 us -> none  [the longest x2 4.32 us: shards(): jnp.zeros((TOKS, channels_in), latents.dtype).at[flat_places]]
    slice x6 -> x0, local copies, waits for them, and re-layouts: 8.48 us -> none  [the longest x2 5.44 us: causal_conv(): kernel = weight[tap_time, tap_row].reshape(3 * channels, outputs)]
    ppermute x4 -> x0, waiting for transfers between devices: 7.91 us -> none  [the longest x2 5.62 us: passed_along(): return lax.ppermute(value, axis, pairs)]
    all_to_all x2 -> x1, starting transfers between devices: 13.4 us -> 7.41 us  [shards(): lax.all_to_all(outgoing.reshape(devices, rows, 128), 'sp', split_axis=0,...]
    ppermute x4 -> x0, starting transfers between devices: 4.7 us -> none  [the longest x1 4.43 us: with_halo(): lax.ppermute(lax.slice_in_dim(block, 0, width, axis=dim), axis, backward)]
    reshape x3 -> x4, local copies, waits for them, and re-layouts: 0.36 us -> 4.99 us  [the longest x1 1.28 us: shards(): b_mid.reshape(1, c_mid)]
  transfers between devices with their start and end apart: 6 -> 1, of which waited for: 3 -> 1; matrix products, arithmetic and copies ran while one was open for 7% -> 14% of each run, Pallas kernels for 0% -> 0%
where the time goes in v1:
time: 44.1 us; the launch traced here: 43.7 us
  Pallas kernels  22.2 us (50%)
  local copies, waits for them, and re-layouts  8.35 us (19%)
  starting transfers between devices  7.41 us (17%)
  waiting for transfers between devices  4.5 us (10%)
  other arithmetic  1.21 us (3%)
    pallas_call x1, Pallas kernels, shards(): pl.pallas_call(functools.partial(main_kernel, devices, blocks), out_shape...  19.7 us
    all_to_all x1, starting transfers between devices, shards(): lax.all_to_all(outgoing.reshape(devices, rows, 128), 'sp', split_axis=0,...  7.41 us
    all_to_all x1, waiting for transfers between devices, shards(): lax.all_to_all(outgoing.reshape(devices, rows, 128), 'sp', split_axis=0,...  4.5 us
    pallas_call x1, Pallas kernels, shards(): pl.pallas_call(functools.partial(pack_kernel, devices, rows, half), out_s...  2.53 us
    unnamed x3, local copies, waits for them, and re-layouts  2.26 us
    reshape x1, local copies, waits for them, and re-layouts, shards(): b_mid.reshape(1, c_mid)  1.28 us
    reshape x1, local copies, waits for them, and re-layouts, shards(): row_cell.reshape(1, tokens)  1.27 us
    reshape x1, local copies, waits for them, and re-layouts, shards(): b_in.reshape(1, c_mid)  1.25 us
  transfers between devices with their start and end apart: 1, of which 1 were waited for; matrix products, arithmetic and copies ran while one was open for 14% of the time, Pallas kernels for 0%

profile of v1, /device:TPU:0, one launch (start us, length us, event | category | flops | bytes accessed | tf_op | source)
XLA Modules:
  0.0 43.7 jit_solution(9849094709533356084)
XLA Ops:
  0.0 1.3 %reshape.24.cells_ref = s32[1,320]{1,0:T(1,128)} reshape(s32[320]{0:T(512)} %param.8) | data formatting | bytes 2560 | tf_op jit(solution)/shard_map/reshape | solution.py:270
  1.3 1.5 %copy.8.latents_ref = bf16[320,64]{1,0:T(8,128)(2,1)} copy(bf16[320,64]{0,1:T(8,128)(2,1)} %param.7) | data formatting | bytes 81920 | tf_op args[0]
  2.8 2.5 %pack.1 = bf16[1152,128]{1,0:T(8,128)(2,1)} custom-call(s32[1,320]{1,0:T(1,128)} %reshape.24.cells_ref, bf16[320,64]{1,0:T(8,128)(2,1)} %copy.8.latents_ref), custom_call_target="tpu_custom_call" | custom-call | tf_op jit(solution)/shard_map/pack/pallas_call | solution.py:264
  5.3 7.4 %all-to-all-start = ((bf16[16,72,128]{2,1,0:T(8,128)(2,1)}), bf16[16,72,128]{2,1,0:T(8,128)(2,1)S(1)}, u32[]{:S(2)}, u32[]{:S(2)}) async-start(bf16[16,72,128]{2,1,0:T(8,128)(2,1)} %bitcast.6), calls=%async_computation | async-start | bytes 589824 | tf_op jit(solution)/shard_map/all_to_all | solution.py:271
  12.7 1.2 %reshape.28.b_in_ref = f32[1,384]{1,0:T(1,128)} reshape(f32[384]{0:T(512)} %param.10) | data formatting | bytes 3072 | tf_op jit(solution)/shard_map/reshape | solution.py:292
  14.0 1.2 %reshape.29.gain_ref = f32[1,384]{1,0:T(1,128)} reshape(f32[384]{0:T(512)} %param.11) | data formatting | bytes 3072 | tf_op jit(solution)/shard_map/reshape | solution.py:293
  15.2 1.3 %reshape.30.b_mid_ref = f32[1,384]{1,0:T(1,128)} reshape(f32[384]{0:T(512)} %param.13) | data formatting | bytes 3072 | tf_op jit(solution)/shard_map/reshape | solution.py:295
  16.5 1.2 %fusion.2 = bf16[3,3,4,16,768]{4,3,2,1,0:T(8,128)(2,1)S(1)} fusion(bf16[3,3,3,16,384]{4,3,2,1,0:T(8,128)(2,1)} %param.9), kind=kLoop, calls=%fused_computation.4 | loop fusion | flops 3538944 | bytes 1216512 | tf_op jit(solution)/shard_map/concatenate | solution.py:251
  17.7 1.1 %pad.6.w_in_ref = bf16[3,256,768]{2,1,0:T(8,128)(2,1)} pad(bf16[3,192,768]{2,1,0:T(8,128)(2,1)S(1)} %bitcast.4, bf16[]{:T(256)} %constant.1.clone.1), padding=0_0x0_64x0_0 | pad | bytes 2064386 | tf_op jit(solution)/shard_map/jit(_pad)/pad | solution.py:252
  18.8 4.5 %all-to-all-done = bf16[16,72,128]{2,1,0:T(8,128)(2,1)S(1)} async-done(((bf16[16,72,128]{2,1,0:T(8,128)(2,1)}), bf16[16,72,128]{2,1,0:T(8,128)(2,1)S(1)}, u32[]{:S(2)}, u32[]{:S(2)}) %all-to-all-start) | async-done | bytes 294944 | tf_op jit(solution)/shard_map/all_to_all | solution.py:271
  23.3 0.0 copy-start
  23.3 0.7 %copy-done = bf16[16,72,128]{2,1,0:T(8,128)(2,1)} copy-done((bf16[16,72,128]{2,1,0:T(8,128)(2,1)}, bf16[16,72,128]{2,1,0:T(8,128)(2,1)S(1)}, u32[]{:S(2)}) %copy-start) | copy-done | bytes 294936
  24.0 19.7 %block.1 = bf16[1280,384]{1,0:T(8,128)(2,1)} custom-call(bf16[1152,128]{1,0:T(8,128)(2,1)} %bitcast.5, bf16[3,256,768]{2,1,0:T(8,128)(2,1)} %pad.6.w_in_ref, f32[1,384]{1,0:T(1,128)} %reshape.28.b_in_ref, f32[1,384]{1,0:T(1,128)} %reshape.29.gain_ref, bf16[3,3,3,384,384]{4,3,2,1,0:T(8,128)(2,1)} %w_mid_hbm.1, f32[1,384]{1,0:T(1,128)} %reshape.30.b_mid_ref), custom_call_target="tpu_custom_call" | custom-call | tf_op jit(solution)/shard_map/block/pallas_call | solution.py:274
Async XLA Ops:
  5.3 18.0 %all-to-all-start = ((bf16[16,72,128]{2,1,0:T(8,128)(2,1)}), bf16[16,72,128]{2,1,0:T(8,128)(2,1)S(1)}, u32[]{:S(2)}, u32[]{:S(2)}) async-start(bf16[16,72,128]{2,1,0:T(8,128)(2,1)} %bitcast.6), calls=%async_computation | async-start | bytes 589824 | tf_op jit(solution)/shard_map/all_to_all | solution.py:271
  23.3 0.7 %copy-start = (bf16[16,72,128]{2,1,0:T(8,128)(2,1)}, bf16[16,72,128]{2,1,0:T(8,128)(2,1)S(1)}, u32[]{:S(2)}) copy-start(bf16[16,72,128]{2,1,0:T(8,128)(2,1)S(1)} %all-to-all-done) | copy-start | bytes 884740

commit v2 on v1

--- a/solution.py
+++ b/solution.py
@@ -20,16 +20,27 @@
 F32 = jnp.float32
 BF16 = jnp.bfloat16
 VMEM = pl.BlockSpec(memory_space=pltpu.VMEM)
-ANY = pl.BlockSpec(memory_space=pl.ANY)
+HBM = pl.BlockSpec(memory_space=pltpu.HBM)
 
 
 def place_code(index):
     return ((index & 127) + 128) << (index >> 7)
 
 
+def select(picks, values):
+    return lax.dot_general(picks, values, (((1,), (1,)), ((), ())), preferred_element_type=F32)
+
+
 def pack_kernel(devices, rows, half, cells_ref, latents_ref, out_ref):
-    tokens = latents_ref.shape[0]
-    cells = cells_ref[...]
+    count = latents_ref.shape[1]
+    tokens = -(-count // 128) * 128
+    cells = cells_ref[...].reshape(1, count)
+    latents = latents_ref[...]
+    if tokens > count:
+        cells = jnp.concatenate([cells, jnp.full((1, tokens - count), 1 << 20, jnp.int32)], 1)
+        latents = jnp.concatenate(
+            [latents, jnp.zeros((latents.shape[0], tokens - count), latents.dtype)], 1
+        )
     column = lax.rem(cells, HALF_W)
     token_row = lax.rem(lax.div(cells, HALF_W), HALF_ROWS * HBANDS)
     frame = lax.div(cells, HALF_W * HALF_ROWS * HBANDS)
@@ -66,15 +77,10 @@
     high = jnp.concatenate(
         [jnp.where(rank[d : d + 1] == high_slot, 1.0, 0.0).astype(BF16) for d in range(devices)], 0
     )
-    latents = latents_ref[...]
     blank = jnp.zeros_like(latents)
-    codes = jnp.transpose(jnp.broadcast_to(code, (128, tokens))).astype(BF16)
-    low_out = jnp.dot(
-        low, jnp.concatenate([latents, blank, codes], 1), preferred_element_type=F32
-    )
-    high_out = jnp.dot(
-        high, jnp.concatenate([blank, latents, codes], 1), preferred_element_type=F32
-    )
+    codes = jnp.broadcast_to(code, (128, tokens)).astype(BF16)
+    low_out = select(low, jnp.concatenate([latents, blank, codes], 0))
+    high_out = select(high, jnp.concatenate([blank, latents, codes], 0))
     row = lax.broadcasted_iota(jnp.int32, (rows, 128), 0)
     diagonal = row == lax.broadcasted_iota(jnp.int32, (rows, 128), 1)
     for d in range(devices):
@@ -87,6 +93,13 @@
         out_ref[part, :] = body.astype(BF16)
 
 
+def weight_kernel(w_ref, sums_ref):
+    first, middle, last = (w_ref[t].astype(F32) * 0.5 for t in range(3))
+    outer = first + last
+    sums_ref[0] = (outer + middle).astype(BF16)
+    sums_ref[1] = (outer - middle).astype(BF16)
+
+
 def main_kernel(
     devices,
     blocks,
@@ -95,20 +108,34 @@
     b_in_ref,
     gain_ref,
     w_mid_hbm,
+    w_sum_hbm,
     b_mid_ref,
-    out_ref,
+    out_hbm,
     w_mid_ref,
     edge_ref,
     active_ref,
+    mixed_ref,
     hidden_ref,
+    sums_ref,
     mix_ref,
+    out_ref,
     w_sem,
+    out_sem,
 ):
-    weights_copy = pltpu.make_async_copy(w_mid_hbm, w_mid_ref, w_sem)
-    weights_copy.start()
+    copies = [
+        pltpu.make_async_copy(source, w_mid_ref.at[k], w_sem.at[k])
+        for k, source in (
+            (1, w_sum_hbm.at[0]),
+            (2, w_sum_hbm.at[1]),
+            (0, w_mid_hbm.at[0]),
+            (3, w_mid_hbm.at[2]),
+        )
+    ]
+    for copy in copies:
+        copy.start()
     total = arrived_ref.shape[0]
     rows = total // devices
-    c_mid = gain_ref.shape[1]
+    c_mid = gain_ref.shape[0]
     tile = lax.rem(lax.axis_index("sp") + OFFSET, devices)
     band = lax.rem(tile, HBANDS)
     time_block = lax.div(tile, HBANDS)
@@ -175,9 +202,11 @@
     index = lax.broadcasted_iota(jnp.int32, (wide, 1), 0)
     global_row = band * HB - 1 + lax.div(index, HALF_W)
     inside = (global_row >= 0) & (global_row < HB * HBANDS)
-    bias = b_in_ref[...]
-    gain = gain_ref[...]
-    for a in range(TB + 2):
+    bias = b_in_ref[...].reshape(1, c_mid)
+    gain = gain_ref[...].reshape(1, c_mid)
+    bias_mid = b_mid_ref[...].reshape(1, c_mid)
+
+    def activate(a):
         windows, kernels = [], []
         for tap in range(3):
             f = TB * (blocks - 1) - 4 + a + tap
@@ -199,48 +228,86 @@
                 hidden_ref[a - 2, :, part] = hidden[HALF_W : HALF_W + HB * HALF_W]
             values = hidden.astype(F32)
             mean = jnp.sum(values * values, 1, keepdims=True) * (1.0 / c_mid)
-            inverse = jnp.where(keep, lax.rsqrt(mean + 1e-06), 0.0)
-            scaled = values * inverse * gain
-            halved = scaled * 0.5
+            inverse = jnp.where(keep, lax.rsqrt(mean + 1e-06) * 0.5, 0.0)
+            halved = values * inverse * gain
             active_ref[a, :, part] = (halved + halved * jnp.tanh(halved)).astype(BF16)
 
-    weights_copy.wait()
     tall = HB * HALF_W
-    for o in range(TB):
+
+    def product(k):
+        if k == 0:
+            mixed_ref[k] = active_ref[0] - active_ref[2]
+        elif k == 1:
+            mixed_ref[k] = active_ref[1] + active_ref[2]
+        elif k == 2:
+            mixed_ref[k] = active_ref[2] - active_ref[1]
+        else:
+            mixed_ref[k] = active_ref[1] - active_ref[3]
         windows, kernels = [], []
         evens, odds, rights, lefts = [], [], [], []
-        for tap_time in range(3):
-            for tap_row in range(3):
-                start = tap_row * HALF_W
-                windows.append(active_ref[o + tap_time, start : start + tall, :])
-                w0, w1, w2 = (w_mid_ref[tap_time, tap_row, t] for t in range(3))
-                kernels.append(jnp.concatenate([w1, w0], 1))
-                kernels.append(jnp.concatenate([w2, w1], 1))
-                evens.append(active_ref[o + tap_time, start : start + tall, :c_mid])
-                odds.append(active_ref[o + tap_time, start : start + tall, c_mid:])
-                rights.append(w2)
-                lefts.append(w0)
-        sums = jnp.dot(
-            jnp.concatenate(windows, 1), jnp.concatenate(kernels, 0), preferred_element_type=F32
-        )
-        from_even = jnp.dot(
-            jnp.concatenate(evens, 1), jnp.concatenate(rights, 0), preferred_element_type=F32
-        ).reshape(HB, HALF_W, c_mid)
-        from_odd = jnp.dot(
-            jnp.concatenate(odds, 1), jnp.concatenate(lefts, 0), preferred_element_type=F32
-        ).reshape(HB, HALF_W, c_mid)
+        for tap_row in range(3):
+            rows_in = slice(tap_row * HALF_W, tap_row * HALF_W + tall)
+            windows.append(mixed_ref[k, rows_in, :])
+            w0, w1, w2 = (w_mid_ref[k, tap_row, t] for t in range(3))
+            kernels.append(jnp.concatenate([w1, w0], 1))
+            kernels.append(jnp.concatenate([w2, w1], 1))
+            evens.append(mixed_ref[k, rows_in, :c_mid])
+            odds.append(mixed_ref[k, rows_in, c_mid:])
+            rights.append(w2)
+            lefts.append(w0)
+        return (
+            jnp.dot(
+                jnp.concatenate(windows, 1),
+                jnp.concatenate(kernels, 0),
+                preferred_element_type=F32,
+            ),
+            jnp.dot(
+                jnp.concatenate(evens, 1), jnp.concatenate(rights, 0), preferred_element_type=F32
+            ),
+            jnp.dot(
+                jnp.concatenate(odds, 1), jnp.concatenate(lefts, 0), preferred_element_type=F32
+            ),
+        )
+
+    def finish(o, sums, from_even, from_odd):
         gap = jnp.zeros((HB, 1, c_mid), F32)
+        from_even = from_even.reshape(HB, HALF_W, c_mid)
+        from_odd = from_odd.reshape(HB, HALF_W, c_mid)
         to_odd = jnp.concatenate([from_even[:, 1:], gap], 1).reshape(tall, c_mid)
         to_even = jnp.concatenate([gap, from_odd[:, :-1]], 1).reshape(tall, c_mid)
         hidden = hidden_ref[o].astype(F32)
-        bias_mid = b_mid_ref[...]
         even_out = sums[:, :c_mid] + to_even + bias_mid + hidden[:, :c_mid]
         odd_out = sums[:, c_mid:] + to_odd + bias_mid + hidden[:, c_mid:]
         for g in range(c_mid // 128):
             part = slice(g * 128, (g + 1) * 128)
             mix_ref[g, pl.ds(0, tall, stride=2), :] = even_out[:, part]
             mix_ref[g, pl.ds(1, tall, stride=2), :] = odd_out[:, part]
-            out_ref[o * 2 * tall : (o + 1) * 2 * tall, part] = mix_ref[g].astype(BF16)
+            out_ref[o, :, part] = mix_ref[g].astype(BF16)
+        copy = pltpu.make_async_copy(
+            out_ref.at[o], out_hbm.at[pl.ds(o * 2 * tall, 2 * tall), :], out_sem.at[o]
+        )
+        copy.start()
+        return copy
+
+    pieces = (slice(0, 2 * c_mid), slice(2 * c_mid, 3 * c_mid), slice(3 * c_mid, 4 * c_mid))
+    activate(1)
+    activate(2)
+    copies[0].wait()
+    for piece, value in zip(pieces, product(1)):
+        sums_ref[0, :, piece] = value
+    activate(0)
+    copies[1].wait()
+    for piece, value in zip(pieces, product(2)):
+        earlier = sums_ref[0, :, piece]
+        sums_ref[0, :, piece] = earlier + value
+        sums_ref[1, :, piece] = earlier - value
+    activate(3)
+    copies[2].wait()
+    first = finish(0, *(sums_ref[0, :, p] + v for p, v in zip(pieces, product(0))))
+    copies[3].wait()
+    last = finish(1, *(sums_ref[1, :, p] - v for p, v in zip(pieces, product(3))))
+    first.wait()
+    last.wait()
 
 
 def input_kernel(w_in):
@@ -267,32 +334,47 @@
         in_specs=[VMEM, VMEM],
         out_specs=VMEM,
         name="pack",
-    )(row_cell.reshape(1, tokens), latents)
+    )(row_cell, latents.T)
     arrived = lax.all_to_all(
         outgoing.reshape(devices, rows, 128), "sp", split_axis=0, concat_axis=0, tiled=True
     )
+    taps = pl.BlockSpec((3, 1, 1, c_mid, c_mid), lambda i, j: (0, i, j, 0, 0))
+    w_sum = pl.pallas_call(
+        weight_kernel,
+        grid=(3, 3),
+        out_shape=jax.ShapeDtypeStruct((2, 3, 3, c_mid, c_mid), BF16),
+        in_specs=[taps],
+        out_specs=pl.BlockSpec((2, 1, 1, c_mid, c_mid), lambda i, j: (0, i, j, 0, 0)),
+        name="weights",
+    )(w_mid)
+    wide = (HB + 2) * HALF_W
     decoded = pl.pallas_call(
         functools.partial(main_kernel, devices, blocks),
         out_shape=jax.ShapeDtypeStruct((TB * HB * W, c_mid), BF16),
-        in_specs=[VMEM, VMEM, VMEM, VMEM, ANY, VMEM],
-        out_specs=VMEM,
+        in_specs=[VMEM, VMEM, VMEM, VMEM, HBM, HBM, VMEM],
+        out_specs=HBM,
         scratch_shapes=[
-            pltpu.VMEM(w_mid.shape, BF16),
+            pltpu.VMEM((4, 3, 3, c_mid, c_mid), BF16),
             pltpu.VMEM((TB * blocks, 2 * (HALF_ROWS + 2) * HALF_W, 128), BF16),
-            pltpu.VMEM((TB + 2, (HB + 2) * HALF_W, 2 * c_mid), BF16),
+            pltpu.VMEM((TB + 2, wide, 2 * c_mid), BF16),
+            pltpu.VMEM((4, wide, 2 * c_mid), BF16),
             pltpu.VMEM((TB, HB * HALF_W, 2 * c_mid), BF16),
+            pltpu.VMEM((2, HB * HALF_W, 4 * c_mid), F32),
             pltpu.VMEM((c_mid // 128, HB * W, 128), F32),
-            pltpu.SemaphoreType.DMA,
+            pltpu.VMEM((TB, HB * W, c_mid), BF16),
+            pltpu.SemaphoreType.DMA((4,)),
+            pltpu.SemaphoreType.DMA((TB,)),
         ],
-        compiler_params=pltpu.CompilerParams(vmem_limit_bytes=56 * 1024 * 1024),
+        compiler_params=pltpu.CompilerParams(vmem_limit_bytes=48 * 1024 * 1024),
         name="block",
     )(
         arrived.reshape(devices * rows, 128),
         input_kernel(w_in),
-        b_in.reshape(1, c_mid),
-        gain.reshape(1, c_mid),
+        b_in,
+        gain,
         w_mid,
-        b_mid.reshape(1, c_mid),
+        w_sum,
+        b_mid,
     )
     return decoded.reshape(1, TB, HB, W, c_mid)
 

time: 44.1 us -> 36.4 us (0.83)
  local copies, waits for them, and re-layouts: 8.35 us -> 0.1 us
  Pallas kernels: 22.2 us -> 27.1 us
  waiting for transfers between devices: 4.5 us -> 1.19 us
  other arithmetic: 1.21 us -> 0.09 us
    pallas_call x0 -> x1, Pallas kernels: none -> 9.13 us  [shards(): pl.pallas_call(weight_kernel, grid=(3, 3), out_shape=jax.ShapeDtypeStruct...]
    reshape x4 -> x0, local copies, waits for them, and re-layouts: 4.99 us -> none  [the longest x1 1.28 us: shards(): b_mid.reshape(1, c_mid)]
    pallas_call x1, Pallas kernels: 19.7 us -> 15.5 us  [shards(): pl.pallas_call(functools.partial(main_kernel, devices, blocks), out_shape...]
    all_to_all x1, waiting for transfers between devices: 4.5 us -> 1.19 us  [shards(): lax.all_to_all(outgoing.reshape(devices, rows, 128), 'sp', split_axis=0,...]
    unnamed x3 -> x8, local copies, waits for them, and re-layouts: 2.26 us -> 0.02 us
    concatenate x1, other arithmetic: 1.21 us -> 0.09 us  [input_kernel(): both = jnp.concatenate([even, odd], -1).reshape(3, 3 * PATCH, 2 * c_mid)]
    pad x1, local copies, waits for them, and re-layouts: 1.1 us -> 0.08 us  [input_kernel(): return jnp.pad(both, ((0, 0), (0, PATCH), (0, 0)))]
  transfers between devices with their start and end apart: 1 -> 1, of which waited for: 1 -> 1; matrix products, arithmetic and copies ran while one was open for 14% -> 0% of each run, Pallas kernels for 0% -> 25%
where the time goes in v2:
time: 36.4 us; the launch traced here: 36 us
  Pallas kernels  27.1 us (74%)
  starting transfers between devices  7.41 us (20%)
  waiting for transfers between devices  1.19 us (3%)
    pallas_call x1, Pallas kernels, shards(): pl.pallas_call(functools.partial(main_kernel, devices, blocks), out_shape...  15.5 us
    pallas_call x1, Pallas kernels, shards(): pl.pallas_call(weight_kernel, grid=(3, 3), out_shape=jax.ShapeDtypeStruct...  9.13 us
    all_to_all x1, starting transfers between devices, shards(): lax.all_to_all(outgoing.reshape(devices, rows, 128), 'sp', split_axis=0,...  7.41 us
    pallas_call x1, Pallas kernels, shards(): pl.pallas_call(functools.partial(pack_kernel, devices, rows, half), out_s...  2.45 us
    all_to_all x1, waiting for transfers between devices, shards(): lax.all_to_all(outgoing.reshape(devices, rows, 128), 'sp', split_axis=0,...  1.19 us
  transfers between devices with their start and end apart: 1, of which 1 were waited for; matrix products, arithmetic and copies ran while one was open for 0% of the time, Pallas kernels for 25%

profile of v2, /device:TPU:0, one launch (start us, length us, event | category | flops | bytes accessed | tf_op | source)
XLA Modules:
  0.0 36.0 jit_solution(9680221492266874119)
XLA Ops:
  0.0 2.5 %pack.1 = bf16[1152,128]{1,0:T(8,128)(2,1)} custom-call(s32[320]{0:T(512)} %cells_ref.1, bf16[64,320]{1,0:T(8,128)(2,1)} %bitcast.8), custom_call_target="tpu_custom_call" | custom-call | tf_op jit(solution)/shard_map/pack/pallas_call | solution.py:331
  2.5 7.4 %all-to-all-start = ((bf16[16,72,128]{2,1,0:T(8,128)(2,1)}), bf16[16,72,128]{2,1,0:T(8,128)(2,1)S(1)}, u32[]{:S(2)}, u32[]{:S(2)}) async-start(bf16[16,72,128]{2,1,0:T(8,128)(2,1)} %bitcast.7), calls=%async_computation | async-start | bytes 589824 | tf_op jit(solution)/shard_map/all_to_all | solution.py:338
  9.9 0.0 copy-start.3
  9.9 9.1 %weights.1.w_sum_hbm = bf16[2,3,3,384,384]{4,3,2,1,0:T(8,128)(2,1)} custom-call(bf16[3,3,3,384,384]{4,3,2,1,0:T(8,128)(2,1)} %w_mid_hbm.1), custom_call_target="tpu_custom_call" | custom-call | tf_op jit(solution)/shard_map/weights/pallas_call | solution.py:342
  19.0 0.0 copy-done.3
  19.0 0.0 copy-start
  19.0 0.0 copy-start.1
  19.0 0.0 copy-start.2
  19.0 0.1 fusion.2
  19.1 0.1 pad.6.w_in_ref
  19.2 1.2 %all-to-all-done = bf16[16,72,128]{2,1,0:T(8,128)(2,1)S(1)} async-done(((bf16[16,72,128]{2,1,0:T(8,128)(2,1)}), bf16[16,72,128]{2,1,0:T(8,128)(2,1)S(1)}, u32[]{:S(2)}, u32[]{:S(2)}) %all-to-all-start) | async-done | bytes 294944 | tf_op jit(solution)/shard_map/all_to_all | solution.py:338
  20.4 0.0 copy-done
  20.4 0.0 copy-done.1
  20.4 0.0 copy-done.2
  20.4 15.5 %block.1 = bf16[1280,384]{1,0:T(8,128)(2,1)} custom-call(bf16[1152,128]{1,0:T(8,128)(2,1)S(1)} %bitcast.5, bf16[3,256,768]{2,1,0:T(8,128)(2,1)S(1)} %pad.6.w_in_ref, f32[384]{0:T(512)S(1)} %copy-done, f32[384]{0:T(512)S(1)} %copy-done.1, bf16[3,3,3,384,384]{4,3,2,1,0:T(8,128)(2,1)} %w_mid_hbm.1, bf16[2,3,3,384,384]{4,3,2,1,0:T(8,128)(2,1)} %weights.1.w_sum_hbm, ...), custom_call_target="tpu_custom_call" | custom-call | tf_op jit(solution)/shard_map/block/pallas_call | solution.py:351
Async XLA Ops:
  2.5 18.0 %all-to-all-start = ((bf16[16,72,128]{2,1,0:T(8,128)(2,1)}), bf16[16,72,128]{2,1,0:T(8,128)(2,1)S(1)}, u32[]{:S(2)}, u32[]{:S(2)}) async-start(bf16[16,72,128]{2,1,0:T(8,128)(2,1)} %bitcast.7), calls=%async_computation | async-start | bytes 589824 | tf_op jit(solution)/shard_map/all_to_all | solution.py:338
  9.9 9.1 %copy-start.3 = (bf16[3,3,3,16,384]{4,3,2,1,0:T(8,128)(2,1)S(1)}, bf16[3,3,3,16,384]{4,3,2,1,0:T(8,128)(2,1)}, u32[]{:S(2)}) copy-start(bf16[3,3,3,16,384]{4,3,2,1,0:T(8,128)(2,1)} %param.9) | copy-start | bytes 995332
  19.0 1.4 %copy-start = (f32[384]{0:T(512)S(1)}, f32[384]{0:T(512)}, u32[]{:S(2)}) copy-start(f32[384]{0:T(512)} %b_in_ref.1) | copy-start | bytes 4612
  19.0 1.4 %copy-start.1 = (f32[384]{0:T(512)S(1)}, f32[384]{0:T(512)}, u32[]{:S(2)}) copy-start(f32[384]{0:T(512)} %gain_ref.1) | copy-start | bytes 4612
  19.0 1.4 %copy-start.2 = (f32[384]{0:T(512)S(1)}, f32[384]{0:T(512)}, u32[]{:S(2)}) copy-start(f32[384]{0:T(512)} %b_mid_ref.1) | copy-start | bytes 4612

commit v3 on v2

v3 whole, which is shorter than its diff:
```python
import functools

import jax
import jax.numpy as jnp
from jax import lax
from jax.experimental import pallas as pl
from jax.experimental.pallas import tpu as pltpu
from jax.sharding import PartitionSpec as P

C_LAT = 16
W = 160
TB = 2
HBANDS = 8
HB = 4
OFFSET = 2 * HBANDS + HBANDS // 2
HALF_ROWS = HB // 2
HALF_W = W // 2
TILE_TOKENS = TB * HALF_ROWS * HALF_W
PATCH = 4 * C_LAT
GROUP = 1
F32 = jnp.float32
BF16 = jnp.bfloat16
VMEM = pl.BlockSpec(memory_space=pltpu.VMEM)
HBM = pl.BlockSpec(memory_space=pltpu.HBM)


def place_code(index):
    return ((index & 127) + 128) << (index >> 7)


def select(picks, values):
    return lax.dot_general(picks, values, (((1,), (1,)), ((), ())), preferred_element_type=F32)


def pack_kernel(devices, rows, half, slots, cells_ref, latents_ref, out_ref):
    chips = devices // GROUP
    count = latents_ref.shape[1]
    tokens = -(-count // 128) * 128
    cells = cells_ref[...].reshape(1, count)
    latents = latents_ref[...]
    if tokens > count:
        cells = jnp.concatenate([cells, jnp.full((1, tokens - count), 1 << 20, jnp.int32)], 1)
        latents = jnp.concatenate(
            [latents, jnp.zeros((latents.shape[0], tokens - count), latents.dtype)], 1
        )
    column = lax.rem(cells, HALF_W)
    token_row = lax.rem(lax.div(cells, HALF_W), HALF_ROWS * HBANDS)
    frame = lax.div(cells, HALF_W * HALF_ROWS * HBANDS)
    block = lax.div(frame, TB)
    band = lax.div(token_row, HALF_ROWS)
    side = lax.rem(token_row, HALF_ROWS)
    local = (lax.rem(frame, TB) * HALF_ROWS + side) * HALF_W + column
    code = place_code((lax.rem(block, 3) * 3 + lax.rem(band, 3)) * TILE_TOKENS + local)
    code = code.astype(F32)

    chip = lax.broadcasted_iota(jnp.int32, (chips, tokens), 0)
    tile = lax.rem(chip * GROUP + OFFSET, devices)
    top = lax.rem(tile, HBANDS)
    bottom = top + GROUP - 1
    age = lax.div(tile, HBANDS) - block
    near = (
        ((band >= top) & (band <= bottom))
        | ((band == top - 1) & (side == HALF_ROWS - 1))
        | ((band == bottom + 1) & (side == 0))
    )
    own = jnp.where(near & (age == 0), 1.0, 0.0)
    old = jnp.where(near & (age > 0) & (age < 3), 1.0, 0.0)
    before = lax.broadcasted_iota(jnp.int32, (tokens, tokens), 0) < lax.broadcasted_iota(
        jnp.int32, (tokens, tokens), 1
    )
    before = jnp.where(before, 1.0, 0.0).astype(BF16)
    ranks = jnp.dot(
        jnp.concatenate([own, old], 0).astype(BF16), before, preferred_element_type=F32
    )
    rank = jnp.where(
        own > 0.5, ranks[:chips], jnp.where(old > 0.5, slots - 1 - ranks[chips:], -1.0)
    )

    slot = lax.broadcasted_iota(jnp.int32, (rows, tokens), 0).astype(F32)
    low_slot = jnp.where(slot < half, slot, -7.0)
    high_slot = jnp.where(slot < half, slot + half, -7.0)
    blank = jnp.zeros_like(latents)
    codes = jnp.broadcast_to(code, (128, tokens)).astype(BF16)
    low_values = jnp.concatenate([latents, blank, codes], 0)
    high_values = jnp.concatenate([blank, latents, codes], 0)
    low_out = select(
        jnp.concatenate(
            [jnp.where(rank[d : d + 1] == low_slot, 1.0, 0.0).astype(BF16) for d in range(chips)], 0
        ),
        low_values,
    )
    high_out = select(
        jnp.concatenate(
            [jnp.where(rank[d : d + 1] == high_slot, 1.0, 0.0).astype(BF16) for d in range(chips)],
            0,
        ),
        high_values,
    )
    row = lax.broadcasted_iota(jnp.int32, (rows, 128), 0)
    diagonal = row == lax.broadcasted_iota(jnp.int32, (rows, 128), 1)
    for d in range(chips):
        part = slice(d * rows, (d + 1) * rows)
        low_codes = jnp.sum(jnp.where(diagonal, low_out[part, 128:], 0.0), 0, keepdims=True)
        high_codes = jnp.sum(jnp.where(diagonal, high_out[part, 128:], 0.0), 0, keepdims=True)
        body = low_out[part, :128] + high_out[part, :128]
        body = jnp.where(row == rows - 2, low_codes, body)
        body = jnp.where(row == rows - 1, high_codes, body)
        out_ref[part, :] = body.astype(BF16)


def weight_kernel(w_ref, sums_ref):
    first, middle, last = (w_ref[t].astype(F32) * 0.5 for t in range(3))
    outer = first + last
    sums_ref[0] = (outer + middle).astype(BF16)
    sums_ref[1] = (outer - middle).astype(BF16)


def slot_pieces(first, last, half, rows):
    pieces = []
    for high, start, stop in (
        (0, first, min(last, half)),
        (1, max(first, half) - half, last - half),
    ):
        if start < stop:
            pieces.append((high, start // 8 * 8, min(rows, -(-stop // 8) * 8)))
    return pieces


def run(*lists):
    steps = []
    for which, steps_of in enumerate(lists):
        for i, step in enumerate(steps_of):
            steps.append(((i + 0.5) / len(steps_of), which, i, step))
    for step in sorted(steps, key=lambda entry: entry[:3]):
        step[3]()


def main_kernel(
    devices,
    blocks,
    rows,
    half,
    own_slots,
    old_slots,
    slots,
    arrived_ref,
    w_in_ref,
    b_in_ref,
    gain_ref,
    w_mid_hbm,
    w_sum_hbm,
    b_mid_ref,
    out_hbm,
    w_mid_ref,
    spread_ref,
    picked_ref,
    placed_ref,
    edge_ref,
    input_ref,
    active_ref,
    mixed_ref,
    hidden_ref,
    sums_ref,
    mix_ref,
    out_ref,
    w_sem,
    out_sem,
):
    def fetch(k, r):
        source, t = ((w_mid_hbm, 0), (w_sum_hbm, 0), (w_sum_hbm, 1), (w_mid_hbm, 2))[k]
        return pltpu.make_async_copy(source.at[t, r], w_mid_ref.at[k, r], w_sem.at[k, r])

    def start_rows(k):
        def body(r, carry):
            fetch(k, r).start()
            return carry

        lax.fori_loop(0, 3, body, 0)

    def wait_rows(k):
        for r in range(3):
            fetch(k, r).wait()

    for k in (1, 0, 2, 3):
        start_rows(k)
    chips = devices // GROUP
    c_mid = gain_ref.shape[0]
    tile = lax.rem(lax.axis_index("sp") + OFFSET, devices)
    band = lax.rem(tile, HBANDS)
    time_block = lax.div(tile, HBANDS)
    token_rows = HALF_ROWS + 2
    wide = (HB + 2) * HALF_W
    tall = HB * HALF_W

    blank = jnp.zeros((C_LAT, c_mid), BF16)
    for tap in range(3):
        for tap_row in range(4):
            for spot in range(4):
                at = slice(tap_row * PATCH + spot * C_LAT, tap_row * PATCH + (spot + 1) * C_LAT)
                even = w_in_ref[tap, tap_row, spot] if tap_row < 3 and spot < 3 else blank
                odd = w_in_ref[tap, tap_row, spot - 1] if tap_row < 3 and spot > 0 else blank
                spread_ref[tap, at, :c_mid] = even
                spread_ref[tap, at, c_mid:] = odd

    k = lax.broadcasted_iota(jnp.int32, (256, 256), 0)
    lane = lax.broadcasted_iota(jnp.int32, (256, 256), 1)
    within = lane & 63
    swap = ((lane >> 6) ^ (lane >> 7)) & 1
    source = swap * (2 * C_LAT) + jnp.where(
        within < C_LAT,
        within + C_LAT,
        jnp.where(within < 3 * C_LAT, within - C_LAT, within - 3 * C_LAT),
    )
    layout = jnp.where((k == source) | (k == source + 128 + PATCH), 1.0, 0.0).astype(BF16)

    def arrivals(pieces):
        codes, tokens = {}, {}
        for high, start, stop in pieces:
            code_row = rows - 2 + high
            codes[high] = jnp.concatenate(
                [
                    arrived_ref[s * rows + code_row : s * rows + code_row + 1, start:stop]
                    for s in range(chips)
                ],
                1,
            ).astype(F32)
            if stop - start == rows:
                parts = [arrived_ref[...]]
            else:
                parts = [
                    arrived_ref[s * rows + start : s * rows + stop, :]
                    for s in range(chips)
                ]
            tokens[high] = jnp.concatenate(parts, 0)
        return codes, tokens

    by_age = [arrivals(slot_pieces(0, own_slots, half, rows))]
    if blocks > 1:
        by_age.append(arrivals(slot_pieces(slots - old_slots, slots, half, rows)))

    column = lax.broadcasted_iota(jnp.int32, (HALF_W, 1), 0)
    lanes = lax.broadcasted_iota(jnp.int32, (1, 1, 256), 2) & 63
    from_left, from_right = lanes < C_LAT, lanes >= 3 * C_LAT
    upper = lax.broadcasted_iota(jnp.int32, (1, 1, 128), 2) < PATCH

    def picks(f):
        if f < 0:
            return []
        frame = (time_block - (blocks - 1)) * TB + f
        codes, tokens = by_age[0 if f >= TB * (blocks - 1) else 1]

        def pick(start, stop):
            def step():
                picked = {}
                for high in codes:
                    picks = []
                    for i in range(start, stop):
                        token_row = band * HALF_ROWS - 1 + i
                        valid = (
                            (frame >= 0) & (token_row >= 0) & (token_row < HALF_ROWS * HBANDS)
                        )
                        frame_in = lax.max(frame, 0)
                        row_in = lax.max(token_row, 0)
                        base = (
                            lax.rem(lax.div(frame_in, TB), 3) * 3
                            + lax.rem(lax.div(row_in, HALF_ROWS), 3)
                        ) * TILE_TOKENS + (
                            lax.rem(frame_in, TB) * HALF_ROWS + lax.rem(row_in, HALF_ROWS)
                        ) * HALF_W
                        code = jnp.where(valid, place_code(base + column), -1).astype(F32)
                        picks.append(jnp.where(codes[high] == code, 1.0, 0.0).astype(BF16))
                    picked[high] = jnp.dot(
                        jnp.concatenate(picks, 0), tokens[high], preferred_element_type=F32
                    ).astype(BF16)
                    picked_ref[f, start * HALF_W : stop * HALF_W, high * 128 : high * 128 + 128] = (
                        picked[high]
                    )
                for high in range(2):
                    if high not in codes:
                        picked_ref[
                            f, start * HALF_W : stop * HALF_W, high * 128 : high * 128 + 128
                        ] = jnp.zeros(((stop - start) * HALF_W, 128), BF16)

            return step

        return [pick(0, token_rows // 2), pick(token_rows // 2, token_rows)]

    def edges(f):
        if f < 0:
            return []

        def spread():
            placed_ref[f] = jnp.dot(picked_ref[f], layout, preferred_element_type=F32)

        def shift():
            placed = placed_ref[f].reshape(token_rows, HALF_W, 256)
            gap = jnp.zeros((token_rows, 1, 256), F32)
            left = jnp.concatenate([gap, placed[:, :-1]], 1)
            right = jnp.concatenate([placed[:, 1:], gap], 1)
            placed = jnp.where(from_left, left, jnp.where(from_right, right, placed))
            even_rows, odd_rows = placed[:, :, :128], placed[:, :, 128:]
            below = jnp.concatenate([odd_rows[1:], jnp.zeros((1, HALF_W, 128), F32)], 0)
            odd_rows = jnp.where(upper, odd_rows, below)
            for i in range(token_rows):
                start = 2 * i * HALF_W
                edge_ref[f, start : start + HALF_W, :] = even_rows[i].astype(BF16)
                edge_ref[f, start + HALF_W : start + 2 * HALF_W, :] = odd_rows[i].astype(BF16)

        return [spread, shift]

    index = lax.broadcasted_iota(jnp.int32, (HALF_W, 1), 0)
    bias = b_in_ref[...].reshape(1, c_mid)
    gain = gain_ref[...].reshape(1, c_mid)
    bias_mid = b_mid_ref[...].reshape(1, c_mid)

    def convolved(a):
        def convolve(part):
            def step():
                windows, kernels = [], []
                for tap in range(3):
                    f = TB * (blocks - 1) - 4 + a + tap
                    if f < 0:
                        continue
                    windows += [
                        edge_ref[f, 0:wide, :],
                        edge_ref[f, 2 * HALF_W : 2 * HALF_W + wide, :],
                    ]
                    kernels.append(spread_ref[tap, :, part])
                input_ref[a, :, part] = jnp.dot(
                    jnp.concatenate(windows, 1),
                    jnp.concatenate(kernels, 0),
                    preferred_element_type=F32,
                )

            return step

        return [convolve(slice(n, n + 256)) for n in range(0, 2 * c_mid, 256)]

    def activated(a):
        def normalise(r, p):
            def step():
                part = slice(p * c_mid, (p + 1) * c_mid)
                at = slice(r * HALF_W, (r + 1) * HALF_W)
                hidden = (input_ref[a, at, part] + bias).astype(BF16)
                if a >= 2 and 1 <= r <= HB:
                    hidden_ref[a - 2, (r - 1) * HALF_W : r * HALF_W, part] = hidden
                values = hidden.astype(F32)
                mean = jnp.sum(values * values, 1, keepdims=True) * (1.0 / c_mid)
                inverse = lax.rsqrt(mean + 1e-06) * 0.5
                keep = time_block * TB - 2 + a >= 0
                if r in (0, HB + 1):
                    row = band * HB - 1 + r
                    keep = keep & (row >= 0) & (row < HB * HBANDS)
                halved = values * jnp.where(keep, inverse, 0.0) * gain
                active_ref[a, at, part] = (halved + halved * jnp.tanh(halved)).astype(BF16)

            return step

        return [normalise(r, p) for r in range(HB + 2) for p in range(2)]

    halves = 2
    part_rows = tall // halves

    def mix(k):
        def rows_of(start):
            def step():
                at = slice(start, start + 2 * HALF_W)
                one, two, sign = ((0, 2, -1), (1, 2, 1), (2, 1, -1), (1, 3, -1))[k]
                first, second = active_ref[one, at, :], active_ref[two, at, :]
                mixed_ref[k, at, :] = first + second if sign > 0 else first - second

            return step

        return [rows_of(start) for start in range(0, wide, 2 * HALF_W)]

    def product(k, h):
        def piece(source, part, kernel):
            def step():
                windows = [
                    mixed_ref[k, r * HALF_W + h * part_rows : r * HALF_W + (h + 1) * part_rows, source]
                    for r in range(3)
                ]
                value = jnp.dot(
                    jnp.concatenate(windows, 1), kernel(), preferred_element_type=F32
                )
                at = slice(h * part_rows, (h + 1) * part_rows)
                if k == 1:
                    sums_ref[1, at, part] = value
                elif k == 0:
                    sums_ref[0, at, part] = sums_ref[1, at, part] + value
                elif k == 2:
                    sums_ref[0, at, part] = sums_ref[0, at, part] + value
                    sums_ref[1, at, part] = sums_ref[1, at, part] - value
                else:
                    sums_ref[1, at, part] = sums_ref[1, at, part] - value

            return step

        def taps(column_tap, start, stop):
            return [w_mid_ref[k, r, column_tap, :, start:stop] for r in range(3)]

        def straight(start, stop):
            def kernel():
                blocks_of = []
                for r in range(3):
                    for even_tap, odd_tap in ((1, 0), (2, 1)):
                        columns = []
                        if start < c_mid:
                            columns.append(
                                w_mid_ref[k, r, even_tap, :, start : min(stop, c_mid)]
                            )
                        if stop > c_mid:
                            columns.append(
                                w_mid_ref[k, r, odd_tap, :, max(start, c_mid) - c_mid : stop - c_mid]
                            )
                        blocks_of.append(
                            columns[0] if len(columns) == 1 else jnp.concatenate(columns, 1)
                        )
                return jnp.concatenate(blocks_of, 0)

            return kernel

        def side(column_tap, start, stop):
            return lambda: jnp.concatenate(taps(column_tap, start, stop), 0)

        steps = [
            piece(slice(0, 2 * c_mid), slice(n, n + 256), straight(n, n + 256))
            for n in range(0, 2 * c_mid, 256)
        ]
        for p, column_tap in ((0, 2), (1, 0)):
            for start in range(0, c_mid, 256):
                stop = min(start + 256, c_mid)
                at = (2 + p) * c_mid
                steps.append(
                    piece(
                        slice(p * c_mid, (p + 1) * c_mid),
                        slice(at + start, at + stop),
                        side(column_tap, start, stop),
                    )
                )
        return steps

    def finish(o, h):
        out_rows = 2 * part_rows

        def lane_group(g):
            def step():
                at = slice(h * part_rows, (h + 1) * part_rows)

                def piece(which):
                    start = which * c_mid + g * 128
                    return sums_ref[o, at, start : start + 128]

                gap = jnp.zeros((HB // halves, 1, 128), F32)
                shape = (HB // halves, HALF_W, 128)
                to_odd = jnp.concatenate([piece(2).reshape(shape)[:, 1:], gap], 1)
                to_even = jnp.concatenate([gap, piece(3).reshape(shape)[:, :-1]], 1)
                lanes_of = slice(g * 128, (g + 1) * 128)
                for p, moved in ((0, to_even), (1, to_odd)):
                    start = p * c_mid + g * 128
                    hidden = hidden_ref[o, at, start : start + 128].astype(F32)
                    mix_ref[o, h, g, pl.ds(p, part_rows, stride=2), :] = (
                        piece(p) + moved.reshape(part_rows, 128) + bias_mid[:, lanes_of] + hidden
                    )
                out_ref[o, h * out_rows : (h + 1) * out_rows, lanes_of] = mix_ref[o, h, g].astype(
                    BF16
                )

            return step

        def send():
            leave(o, h).start()

        return [lane_group(g) for g in range(c_mid // 128)] + [send]

    def leave(o, h):
        out_rows = 2 * part_rows
        return pltpu.make_async_copy(
            out_ref.at[o, pl.ds(h * out_rows, out_rows), :],
            out_hbm.at[pl.ds(o * 2 * tall + h * out_rows, out_rows), :],
            out_sem.at[o, h],
        )

    newest = TB * (blocks - 1) - 2
    for f in range(newest):
        run(picks(f) + edges(f))
    run(picks(newest) + picks(newest + 1))
    run(edges(newest), picks(newest + 2))
    run(edges(newest + 1) + convolved(1), picks(newest + 3))
    run(edges(newest + 2) + convolved(2), activated(1))
    run(edges(newest + 3) + convolved(0) + convolved(3), activated(2))
    wait_rows(1)
    wait_rows(0)
    run(mix(1))
    run(product(1, 0) + product(1, 1), activated(0) + mix(0))
    run(product(0, 0) + product(0, 1), mix(2))
    wait_rows(2)
    wait_rows(3)
    run(product(2, 0) + product(2, 1), activated(3) + mix(3))
    run(product(3, 0), finish(0, 0) + finish(0, 1))
    run(product(3, 1), finish(1, 0))
    run(finish(1, 1))
    for o in range(TB):
        for h in range(halves):
            leave(o, h).wait()


def shards(latents, row_cell, w_in, b_in, gain, w_mid, b_mid):
    devices = lax.axis_size("sp")
    tokens = latents.shape[0]
    c_mid = gain.shape[0]
    blocks = min(3, devices // HBANDS)
    chips = devices // GROUP
    pair = tokens // devices
    bands = GROUP + 2
    own_slots = pair * bands + pair
    old_slots = pair * bands * (blocks - 1) + pair
    slots = pair * bands * blocks + pair
    half = -(-slots // 2)
    rows = -(-(half + 2) // 8) * 8
    outgoing = pl.pallas_call(
        functools.partial(pack_kernel, devices, rows, half, slots),
        out_shape=jax.ShapeDtypeStruct((chips * rows, 128), BF16),
        in_specs=[VMEM, VMEM],
        out_specs=VMEM,
        name="pack",
    )(row_cell, latents.T)
    arrived = lax.all_to_all(
        outgoing.reshape(chips, rows, 128), "sp", split_axis=0, concat_axis=0, tiled=True
    )
    w_sum = pl.pallas_call(
        weight_kernel,
        grid=(3, 3),
        out_shape=jax.ShapeDtypeStruct((2, 3, 3, c_mid, c_mid), BF16),
        in_specs=[pl.BlockSpec((3, 1, 1, c_mid, c_mid), lambda i, j: (0, i, j, 0, 0))],
        out_specs=pl.BlockSpec((2, 1, 1, c_mid, c_mid), lambda i, j: (0, i, j, 0, 0)),
        name="weights",
    )(w_mid)
    wide = (HB + 2) * HALF_W
    tall = HB * HALF_W
    frames = TB * blocks
    decoded = pl.pallas_call(
        functools.partial(
            main_kernel, devices, blocks, rows, half, own_slots, old_slots, slots
        ),
        out_shape=jax.ShapeDtypeStruct((TB * HB * W, c_mid), BF16),
        in_specs=[VMEM, VMEM, VMEM, VMEM, HBM, HBM, VMEM],
        out_specs=HBM,
        scratch_shapes=[
            pltpu.VMEM((4, 3, 3, c_mid, c_mid), BF16),
            pltpu.VMEM((3, 4 * PATCH, 2 * c_mid), BF16),
            pltpu.VMEM((frames, (HALF_ROWS + 2) * HALF_W, 256), BF16),
            pltpu.VMEM((frames, (HALF_ROWS + 2) * HALF_W, 256), F32),
            pltpu.VMEM((frames, 2 * (HALF_ROWS + 2) * HALF_W, 128), BF16),
            pltpu.VMEM((TB + 2, wide, 2 * c_mid), F32),
            pltpu.VMEM((TB + 2, wide, 2 * c_mid), BF16),
            pltpu.VMEM((4, wide, 2 * c_mid), BF16),
            pltpu.VMEM((TB, tall, 2 * c_mid), BF16),
            pltpu.VMEM((2, tall, 4 * c_mid), F32),
            pltpu.VMEM((TB, 2, c_mid // 128, tall, 128), F32),
            pltpu.VMEM((TB, 2 * tall, c_mid), BF16),
            pltpu.SemaphoreType.DMA((4, 3)),
            pltpu.SemaphoreType.DMA((TB, 2)),
        ],
        compiler_params=pltpu.CompilerParams(vmem_limit_bytes=48 * 1024 * 1024),
        name="block",
    )(
        arrived.reshape(chips * rows, 128),
        w_in,
        b_in,
        gain,
        w_mid,
        pltpu.with_memory_space_constraint(w_sum, pltpu.HBM),
        b_mid,
    )
    return decoded.reshape(1, TB, HB, W, c_mid)


def solution(mesh):
    return jax.shard_map(
        shards,
        mesh=mesh,
        in_specs=(P(("grp", "sp"), None), P(("grp", "sp")), P(), P(), P(), P(), P()),
        out_specs=P(("grp", "sp"), None, None, None, None),
        check_vma=False,
    )
```

time: 36.4 us -> 34.8 us (0.956)
  Pallas kernels: 27.1 us -> 25.5 us
    pallas_call x2, Pallas kernels: 18 us -> 16.4 us  [the longest x1 13.9 us: shards(): pl.pallas_call(functools.partial(main_kernel, devices, blocks, rows, half...]
  transfers between devices with their start and end apart: 1 -> 1, of which waited for: 1 -> 1; matrix products, arithmetic and copies ran while one was open for 0% -> 0% of each run, Pallas kernels for 25% -> 27%
where the time goes in v3:
time: 34.8 us; the launch traced here: 34.4 us
  Pallas kernels  25.5 us (73%)
  starting transfers between devices  7.43 us (21%)
  waiting for transfers between devices  1.42 us (4%)
    pallas_call x1, Pallas kernels, shards(): pl.pallas_call(functools.partial(main_kernel, devices, blocks, rows, half...  13.9 us
    pallas_call x1, Pallas kernels, shards(): pl.pallas_call(weight_kernel, grid=(3, 3), out_shape=jax.ShapeDtypeStruct...  9.12 us
    all_to_all x1, starting transfers between devices, shards(): lax.all_to_all(outgoing.reshape(chips, rows, 128), 'sp', split_axis=0, co...  7.43 us
    pallas_call x1, Pallas kernels, shards(): pl.pallas_call(functools.partial(pack_kernel, devices, rows, half, slots)...  2.51 us
    all_to_all x1, waiting for transfers between devices, shards(): lax.all_to_all(outgoing.reshape(chips, rows, 128), 'sp', split_axis=0, co...  1.42 us
  transfers between devices with their start and end apart: 1, of which 1 were waited for; matrix products, arithmetic and copies ran while one was open for 0% of the time, Pallas kernels for 27%

profile of v3, /device:TPU:0, one launch (start us, length us, event | category | flops | bytes accessed | tf_op | source)
XLA Modules:
  0.0 34.4 jit_solution(4818421807617406639)
XLA Ops:
  0.0 0.0 copy-start.3
  0.0 0.0 copy-start.2
  0.0 0.0 copy-start.1
  0.0 0.0 copy-start
  0.0 2.5 %pack.1 = bf16[1152,128]{1,0:T(8,128)(2,1)} custom-call(s32[320]{0:T(512)} %cells_ref.1, bf16[64,320]{1,0:T(8,128)(2,1)} %bitcast.6), custom_call_target="tpu_custom_call" | custom-call | tf_op jit(solution)/shard_map/pack/pallas_call | solution.py:521
  2.5 7.4 %all-to-all-start = ((bf16[16,72,128]{2,1,0:T(8,128)(2,1)}), bf16[16,72,128]{2,1,0:T(8,128)(2,1)S(1)}, u32[]{:S(2)}, u32[]{:S(2)}) async-start(bf16[16,72,128]{2,1,0:T(8,128)(2,1)} %bitcast.5), calls=%async_computation | async-start | bytes 589824 | tf_op jit(solution)/shard_map/all_to_all | solution.py:528
  10.0 9.1 %weights.1.w_sum_hbm = bf16[2,3,3,384,384]{4,3,2,1,0:T(8,128)(2,1)} custom-call(bf16[3,3,3,384,384]{4,3,2,1,0:T(8,128)(2,1)} %w_mid_hbm.1), custom_call_target="tpu_custom_call" | custom-call | tf_op jit(solution)/shard_map/weights/pallas_call | solution.py:531
  19.1 1.4 %all-to-all-done = bf16[16,72,128]{2,1,0:T(8,128)(2,1)S(1)} async-done(((bf16[16,72,128]{2,1,0:T(8,128)(2,1)}), bf16[16,72,128]{2,1,0:T(8,128)(2,1)S(1)}, u32[]{:S(2)}, u32[]{:S(2)}) %all-to-all-start) | async-done | bytes 294944 | tf_op jit(solution)/shard_map/all_to_all | solution.py:528
  20.5 0.0 copy-done.3
  20.5 0.0 copy-done.2
  20.5 0.0 copy-done.1
  20.5 0.0 copy-done
  20.5 13.9 %block.1 = bf16[1280,384]{1,0:T(8,128)(2,1)} custom-call(bf16[1152,128]{1,0:T(8,128)(2,1)S(1)} %bitcast.4, bf16[3,3,3,16,384]{4,3,2,1,0:T(8,128)(2,1)S(1)} %copy-done, f32[384]{0:T(512)S(1)} %copy-done.1, f32[384]{0:T(512)S(1)} %copy-done.2, bf16[3,3,3,384,384]{4,3,2,1,0:T(8,128)(2,1)} %w_mid_hbm.1, bf16[2,3,3,384,384]{4,3,2,1,0:T(8,128)(2,1)} %weights.1.w_sum_hbm, ...), custom_call_target="tpu_custom_call" | custom-call | tf_op jit(solution)/shard_map/block/pallas_call | solution.py:542
Async XLA Ops:
  0.0 20.5 %copy-start.3 = (f32[384]{0:T(512)S(1)}, f32[384]{0:T(512)}, u32[]{:S(2)}) copy-start(f32[384]{0:T(512)} %b_mid_ref.1) | copy-start | bytes 4612
  0.0 20.5 %copy-start.2 = (f32[384]{0:T(512)S(1)}, f32[384]{0:T(512)}, u32[]{:S(2)}) copy-start(f32[384]{0:T(512)} %gain_ref.1) | copy-start | bytes 4612
  0.0 20.5 %copy-start.1 = (f32[384]{0:T(512)S(1)}, f32[384]{0:T(512)}, u32[]{:S(2)}) copy-start(f32[384]{0:T(512)} %b_in_ref.1) | copy-start | bytes 4612
  0.0 20.5 %copy-start = (bf16[3,3,3,16,384]{4,3,2,1,0:T(8,128)(2,1)S(1)}, bf16[3,3,3,16,384]{4,3,2,1,0:T(8,128)(2,1)}, u32[]{:S(2)}) copy-start(bf16[3,3,3,16,384]{4,3,2,1,0:T(8,128)(2,1)} %w_in_ref.1) | copy-start | bytes 995332
  2.5 18.0 %all-to-all-start = ((bf16[16,72,128]{2,1,0:T(8,128)(2,1)}), bf16[16,72,128]{2,1,0:T(8,128)(2,1)S(1)}, u32[]{:S(2)}, u32[]{:S(2)}) async-start(bf16[16,72,128]{2,1,0:T(8,128)(2,1)} %bitcast.5), calls=%async_computation | async-start | bytes 589824 | tf_op jit(solution)/shard_map/all_to_all | solution.py:528

commit v4 on v3

--- a/solution.py
+++ b/solution.py
@@ -423,22 +423,34 @@
         def side(column_tap, start, stop):
             return lambda: jnp.concatenate(taps(column_tap, start, stop), 0)
 
-        steps = [
-            piece(slice(0, 2 * c_mid), slice(n, n + 256), straight(n, n + 256))
-            for n in range(0, 2 * c_mid, 256)
+        def both_sides(start):
+            def kernel():
+                width = c_mid - start
+                gap = jnp.zeros((c_mid, width), BF16)
+                blocks_of = []
+                for right, left in zip(taps(2, start, c_mid), taps(0, start, c_mid)):
+                    blocks_of.append(jnp.concatenate([right, gap], 1))
+                    blocks_of.append(jnp.concatenate([gap, left], 1))
+                return jnp.concatenate(blocks_of, 0)
+
+            return kernel
+
+        whole = slice(0, 2 * c_mid)
+        straights = [
+            piece(whole, slice(n, n + 256), straight(n, n + 256)) for n in range(0, 2 * c_mid, 256)
         ]
-        for p, column_tap in ((0, 2), (1, 0)):
-            for start in range(0, c_mid, 256):
-                stop = min(start + 256, c_mid)
-                at = (2 + p) * c_mid
-                steps.append(
-                    piece(
-                        slice(p * c_mid, (p + 1) * c_mid),
-                        slice(at + start, at + stop),
-                        side(column_tap, start, stop),
-                    )
-                )
-        return steps
+        full = c_mid // 256 * 256
+        sides = [
+            piece(slice(0, c_mid), slice(2 * c_mid, 2 * c_mid + full), side(2, 0, full)),
+            piece(
+                slice(c_mid, 2 * c_mid), slice(2 * c_mid + full, 2 * c_mid + 2 * full), side(0, 0, full)
+            ),
+            piece(whole, slice(2 * c_mid + 2 * full, 4 * c_mid), both_sides(full)),
+        ]
+        return straights[:2] + sides[:2] + straights[2:] + sides[2:]
+
+    full = c_mid // 256 * 256
+    rest = c_mid - full
 
     def finish(o, h):
         out_rows = 2 * part_rows
@@ -446,39 +458,46 @@
         def lane_group(g):
             def step():
                 at = slice(h * part_rows, (h + 1) * part_rows)
-
-                def piece(which):
-                    start = which * c_mid + g * 128
+                lanes_of = slice(g * 128, (g + 1) * 128)
+
+                def columns(start):
                     return sums_ref[o, at, start : start + 128]
 
+                if g * 128 < full:
+                    right = 2 * c_mid + g * 128
+                    left = right + full
+                else:
+                    right = 2 * c_mid + 2 * full + g * 128 - full
+                    left = right + rest
                 gap = jnp.zeros((HB // halves, 1, 128), F32)
                 shape = (HB // halves, HALF_W, 128)
-                to_odd = jnp.concatenate([piece(2).reshape(shape)[:, 1:], gap], 1)
-                to_even = jnp.concatenate([gap, piece(3).reshape(shape)[:, :-1]], 1)
-                lanes_of = slice(g * 128, (g + 1) * 128)
+                to_odd = jnp.concatenate([columns(right).reshape(shape)[:, 1:], gap], 1)
+                to_even = jnp.concatenate([gap, columns(left).reshape(shape)[:, :-1]], 1)
                 for p, moved in ((0, to_even), (1, to_odd)):
                     start = p * c_mid + g * 128
                     hidden = hidden_ref[o, at, start : start + 128].astype(F32)
                     mix_ref[o, h, g, pl.ds(p, part_rows, stride=2), :] = (
-                        piece(p) + moved.reshape(part_rows, 128) + bias_mid[:, lanes_of] + hidden
+                        columns(start)
+                        + moved.reshape(part_rows, 128)
+                        + bias_mid[:, lanes_of]
+                        + hidden
                     )
                 out_ref[o, h * out_rows : (h + 1) * out_rows, lanes_of] = mix_ref[o, h, g].astype(
                     BF16
                 )
+                leave(o, h, g).start()
 
             return step
 
-        def send():
-            leave(o, h).start()
-
-        return [lane_group(g) for g in range(c_mid // 128)] + [send]
-
-    def leave(o, h):
+        return [lane_group(g) for g in range(c_mid // 128)]
+
+    def leave(o, h, g):
         out_rows = 2 * part_rows
+        lanes_of = pl.ds(g * 128, 128)
         return pltpu.make_async_copy(
-            out_ref.at[o, pl.ds(h * out_rows, out_rows), :],
-            out_hbm.at[pl.ds(o * 2 * tall + h * out_rows, out_rows), :],
-            out_sem.at[o, h],
+            out_ref.at[o, pl.ds(h * out_rows, out_rows), lanes_of],
+            out_hbm.at[pl.ds(o * 2 * tall + h * out_rows, out_rows), lanes_of],
+            out_sem.at[o, h, g],
         )
 
     newest = TB * (blocks - 1) - 2
@@ -489,20 +508,20 @@
     run(edges(newest + 1) + convolved(1), picks(newest + 3))
     run(edges(newest + 2) + convolved(2), activated(1))
     run(edges(newest + 3) + convolved(0) + convolved(3), activated(2))
-    wait_rows(1)
-    wait_rows(0)
+    for k in range(4):
+        wait_rows(k)
     run(mix(1))
     run(product(1, 0) + product(1, 1), activated(0) + mix(0))
     run(product(0, 0) + product(0, 1), mix(2))
-    wait_rows(2)
-    wait_rows(3)
     run(product(2, 0) + product(2, 1), activated(3) + mix(3))
     run(product(3, 0), finish(0, 0) + finish(0, 1))
-    run(product(3, 1), finish(1, 0))
-    run(finish(1, 1))
+    last = finish(1, 1)
+    run(product(3, 1)[:4], finish(1, 0))
+    run(last[:1] + product(3, 1)[4:5] + last[1:2] + product(3, 1)[5:] + last[2:])
     for o in range(TB):
         for h in range(halves):
-            leave(o, h).wait()
+            for g in range(c_mid // 128):
+                leave(o, h, g).wait()
 
 
 def shards(latents, row_cell, w_in, b_in, gain, w_mid, b_mid):
@@ -560,7 +579,7 @@
             pltpu.VMEM((TB, 2, c_mid // 128, tall, 128), F32),
             pltpu.VMEM((TB, 2 * tall, c_mid), BF16),
             pltpu.SemaphoreType.DMA((4, 3)),
-            pltpu.SemaphoreType.DMA((TB, 2)),
+            pltpu.SemaphoreType.DMA((TB, 2, c_mid // 128)),
         ],
         compiler_params=pltpu.CompilerParams(vmem_limit_bytes=48 * 1024 * 1024),
         name="block",

time: 34.8 us -> 34.6 us (level)
  no operation moved by 1% of the time
where the time goes in v4:
time: 34.6 us; the launch traced here: 34.1 us
  Pallas kernels  25.2 us (73%)
  starting transfers between devices  7.43 us (21%)
  waiting for transfers between devices  1.42 us (4%)
    pallas_call x1, Pallas kernels, shards(): pl.pallas_call(functools.partial(main_kernel, devices, blocks, rows, half...  13.6 us
    pallas_call x1, Pallas kernels, shards(): pl.pallas_call(weight_kernel, grid=(3, 3), out_shape=jax.ShapeDtypeStruct...  9.12 us
    all_to_all x1, starting transfers between devices, shards(): lax.all_to_all(outgoing.reshape(chips, rows, 128), 'sp', split_axis=0, co...  7.43 us
    pallas_call x1, Pallas kernels, shards(): pl.pallas_call(functools.partial(pack_kernel, devices, rows, half, slots)...  2.51 us
    all_to_all x1, waiting for transfers between devices, shards(): lax.all_to_all(outgoing.reshape(chips, rows, 128), 'sp', split_axis=0, co...  1.42 us
  transfers between devices with their start and end apart: 1, of which 1 were waited for; matrix products, arithmetic and copies ran while one was open for 0% of the time, Pallas kernels for 27%

profile of v4, /device:TPU:0, one launch (start us, length us, event | category | flops | bytes accessed | tf_op | source)
XLA Modules:
  0.0 34.1 jit_solution(5088756612550142488)
XLA Ops:
  0.0 0.0 copy-start.3
  0.0 0.0 copy-start.2
  0.0 0.0 copy-start.1
  0.0 0.0 copy-start
  0.0 2.5 %pack.1 = bf16[1152,128]{1,0:T(8,128)(2,1)} custom-call(s32[320]{0:T(512)} %cells_ref.1, bf16[64,320]{1,0:T(8,128)(2,1)} %bitcast.6), custom_call_target="tpu_custom_call" | custom-call | tf_op jit(solution)/shard_map/pack/pallas_call | solution.py:540
  2.5 7.4 %all-to-all-start = ((bf16[16,72,128]{2,1,0:T(8,128)(2,1)}), bf16[16,72,128]{2,1,0:T(8,128)(2,1)S(1)}, u32[]{:S(2)}, u32[]{:S(2)}) async-start(bf16[16,72,128]{2,1,0:T(8,128)(2,1)} %bitcast.5), calls=%async_computation | async-start | bytes 589824 | tf_op jit(solution)/shard_map/all_to_all | solution.py:547
  10.0 9.1 %weights.1.w_sum_hbm = bf16[2,3,3,384,384]{4,3,2,1,0:T(8,128)(2,1)} custom-call(bf16[3,3,3,384,384]{4,3,2,1,0:T(8,128)(2,1)} %w_mid_hbm.1), custom_call_target="tpu_custom_call" | custom-call | tf_op jit(solution)/shard_map/weights/pallas_call | solution.py:550
  19.1 1.4 %all-to-all-done = bf16[16,72,128]{2,1,0:T(8,128)(2,1)S(1)} async-done(((bf16[16,72,128]{2,1,0:T(8,128)(2,1)}), bf16[16,72,128]{2,1,0:T(8,128)(2,1)S(1)}, u32[]{:S(2)}, u32[]{:S(2)}) %all-to-all-start) | async-done | bytes 294944 | tf_op jit(solution)/shard_map/all_to_all | solution.py:547
  20.5 0.0 copy-done.3
  20.5 0.0 copy-done.2
  20.5 0.0 copy-done.1
  20.5 0.0 copy-done
  20.5 13.6 %block.1 = bf16[1280,384]{1,0:T(8,128)(2,1)} custom-call(bf16[1152,128]{1,0:T(8,128)(2,1)S(1)} %bitcast.4, bf16[3,3,3,16,384]{4,3,2,1,0:T(8,128)(2,1)S(1)} %copy-done, f32[384]{0:T(512)S(1)} %copy-done.1, f32[384]{0:T(512)S(1)} %copy-done.2, bf16[3,3,3,384,384]{4,3,2,1,0:T(8,128)(2,1)} %w_mid_hbm.1, bf16[2,3,3,384,384]{4,3,2,1,0:T(8,128)(2,1)} %weights.1.w_sum_hbm, ...), custom_call_target="tpu_custom_call" | custom-call | tf_op jit(solution)/shard_map/block/pallas_call | solution.py:561
Async XLA Ops:
  0.0 20.5 %copy-start.3 = (f32[384]{0:T(512)S(1)}, f32[384]{0:T(512)}, u32[]{:S(2)}) copy-start(f32[384]{0:T(512)} %b_mid_ref.1) | copy-start | bytes 4612
  0.0 20.5 %copy-start.2 = (f32[384]{0:T(512)S(1)}, f32[384]{0:T(512)}, u32[]{:S(2)}) copy-start(f32[384]{0:T(512)} %gain_ref.1) | copy-start | bytes 4612
  0.0 20.5 %copy-start.1 = (f32[384]{0:T(512)S(1)}, f32[384]{0:T(512)}, u32[]{:S(2)}) copy-start(f32[384]{0:T(512)} %b_in_ref.1) | copy-start | bytes 4612
  0.0 20.5 %copy-start = (bf16[3,3,3,16,384]{4,3,2,1,0:T(8,128)(2,1)S(1)}, bf16[3,3,3,16,384]{4,3,2,1,0:T(8,128)(2,1)}, u32[]{:S(2)}) copy-start(bf16[3,3,3,16,384]{4,3,2,1,0:T(8,128)(2,1)} %w_in_ref.1) | copy-start | bytes 995332
  2.5 18.0 %all-to-all-start = ((bf16[16,72,128]{2,1,0:T(8,128)(2,1)}), bf16[16,72,128]{2,1,0:T(8,128)(2,1)S(1)}, u32[]{:S(2)}, u32[]{:S(2)}) async-start(bf16[16,72,128]{2,1,0:T(8,128)(2,1)} %bitcast.5), calls=%async_computation | async-start | bytes 589824 | tf_op jit(solution)/shard_map/all_to_all | solution.py:547

commit v5 on v4

--- a/solution.py
+++ b/solution.py
@@ -223,7 +223,7 @@
                     for s in range(chips)
                 ],
                 1,
-            ).astype(F32)
+            )
             if stop - start == rows:
                 parts = [arrived_ref[...]]
             else:
@@ -238,6 +238,7 @@
     if blocks > 1:
         by_age.append(arrivals(slot_pieces(slots - old_slots, slots, half, rows)))
 
+    one, zero = jnp.ones((), BF16), jnp.zeros((), BF16)
     column = lax.broadcasted_iota(jnp.int32, (HALF_W, 1), 0)
     lanes = lax.broadcasted_iota(jnp.int32, (1, 1, 256), 2) & 63
     from_left, from_right = lanes < C_LAT, lanes >= 3 * C_LAT
@@ -267,8 +268,8 @@
                         ) * TILE_TOKENS + (
                             lax.rem(frame_in, TB) * HALF_ROWS + lax.rem(row_in, HALF_ROWS)
                         ) * HALF_W
-                        code = jnp.where(valid, place_code(base + column), -1).astype(F32)
-                        picks.append(jnp.where(codes[high] == code, 1.0, 0.0).astype(BF16))
+                        code = jnp.where(valid, place_code(base + column), -1).astype(F32).astype(BF16)
+                        picks.append(jnp.where(codes[high] == code, one, zero))
                     picked[high] = jnp.dot(
                         jnp.concatenate(picks, 0), tokens[high], preferred_element_type=F32
                     ).astype(BF16)

time: 34.6 us -> 34.5 us (level)
  no operation moved by 1% of the time
where the time goes in v5:
time: 34.5 us; the launch traced here: 34.1 us
  Pallas kernels  25.2 us (73%)
  starting transfers between devices  7.43 us (22%)
  waiting for transfers between devices  1.42 us (4%)
    pallas_call x1, Pallas kernels, shards(): pl.pallas_call(functools.partial(main_kernel, devices, blocks, rows, half...  13.6 us
    pallas_call x1, Pallas kernels, shards(): pl.pallas_call(weight_kernel, grid=(3, 3), out_shape=jax.ShapeDtypeStruct...  9.12 us
    all_to_all x1, starting transfers between devices, shards(): lax.all_to_all(outgoing.reshape(chips, rows, 128), 'sp', split_axis=0, co...  7.43 us
    pallas_call x1, Pallas kernels, shards(): pl.pallas_call(functools.partial(pack_kernel, devices, rows, half, slots)...  2.51 us
    all_to_all x1, waiting for transfers between devices, shards(): lax.all_to_all(outgoing.reshape(chips, rows, 128), 'sp', split_axis=0, co...  1.42 us
  transfers between devices with their start and end apart: 1, of which 1 were waited for; matrix products, arithmetic and copies ran while one was open for 0% of the time, Pallas kernels for 27%

profile of v5, /device:TPU:0, one launch (start us, length us, event | category | flops | bytes accessed | tf_op | source)
XLA Modules:
  0.0 34.1 jit_solution(4032697140958500013)
XLA Ops:
  0.0 0.0 copy-start.3
  0.0 0.0 copy-start.2
  0.0 0.0 copy-start.1
  0.0 0.0 copy-start
  0.0 2.5 %pack.1 = bf16[1152,128]{1,0:T(8,128)(2,1)} custom-call(s32[320]{0:T(512)} %cells_ref.1, bf16[64,320]{1,0:T(8,128)(2,1)} %bitcast.6), custom_call_target="tpu_custom_call" | custom-call | tf_op jit(solution)/shard_map/pack/pallas_call | solution.py:541
  2.5 7.4 %all-to-all-start = ((bf16[16,72,128]{2,1,0:T(8,128)(2,1)}), bf16[16,72,128]{2,1,0:T(8,128)(2,1)S(1)}, u32[]{:S(2)}, u32[]{:S(2)}) async-start(bf16[16,72,128]{2,1,0:T(8,128)(2,1)} %bitcast.5), calls=%async_computation | async-start | bytes 589824 | tf_op jit(solution)/shard_map/all_to_all | solution.py:548
  10.0 9.1 %weights.1.w_sum_hbm = bf16[2,3,3,384,384]{4,3,2,1,0:T(8,128)(2,1)} custom-call(bf16[3,3,3,384,384]{4,3,2,1,0:T(8,128)(2,1)} %w_mid_hbm.1), custom_call_target="tpu_custom_call" | custom-call | tf_op jit(solution)/shard_map/weights/pallas_call | solution.py:551
  19.1 1.4 %all-to-all-done = bf16[16,72,128]{2,1,0:T(8,128)(2,1)S(1)} async-done(((bf16[16,72,128]{2,1,0:T(8,128)(2,1)}), bf16[16,72,128]{2,1,0:T(8,128)(2,1)S(1)}, u32[]{:S(2)}, u32[]{:S(2)}) %all-to-all-start) | async-done | bytes 294944 | tf_op jit(solution)/shard_map/all_to_all | solution.py:548
  20.5 0.0 copy-done.3
  20.5 0.0 copy-done.2
  20.5 0.0 copy-done.1
  20.5 0.0 copy-done
  20.5 13.6 %block.1 = bf16[1280,384]{1,0:T(8,128)(2,1)} custom-call(bf16[1152,128]{1,0:T(8,128)(2,1)S(1)} %bitcast.4, bf16[3,3,3,16,384]{4,3,2,1,0:T(8,128)(2,1)S(1)} %copy-done, f32[384]{0:T(512)S(1)} %copy-done.1, f32[384]{0:T(512)S(1)} %copy-done.2, bf16[3,3,3,384,384]{4,3,2,1,0:T(8,128)(2,1)} %w_mid_hbm.1, bf16[2,3,3,384,384]{4,3,2,1,0:T(8,128)(2,1)} %weights.1.w_sum_hbm, ...), custom_call_target="tpu_custom_call" | custom-call | tf_op jit(solution)/shard_map/block/pallas_call | solution.py:562
Async XLA Ops:
  0.0 20.5 %copy-start.3 = (f32[384]{0:T(512)S(1)}, f32[384]{0:T(512)}, u32[]{:S(2)}) copy-start(f32[384]{0:T(512)} %b_mid_ref.1) | copy-start | bytes 4612
  0.0 20.5 %copy-start.2 = (f32[384]{0:T(512)S(1)}, f32[384]{0:T(512)}, u32[]{:S(2)}) copy-start(f32[384]{0:T(512)} %gain_ref.1) | copy-start | bytes 4612
  0.0 20.5 %copy-start.1 = (f32[384]{0:T(512)S(1)}, f32[384]{0:T(512)}, u32[]{:S(2)}) copy-start(f32[384]{0:T(512)} %b_in_ref.1) | copy-start | bytes 4612
  0.0 20.5 %copy-start = (bf16[3,3,3,16,384]{4,3,2,1,0:T(8,128)(2,1)S(1)}, bf16[3,3,3,16,384]{4,3,2,1,0:T(8,128)(2,1)}, u32[]{:S(2)}) copy-start(bf16[3,3,3,16,384]{4,3,2,1,0:T(8,128)(2,1)} %w_in_ref.1) | copy-start | bytes 995332
  2.5 18.0 %all-to-all-start = ((bf16[16,72,128]{2,1,0:T(8,128)(2,1)}), bf16[16,72,128]{2,1,0:T(8,128)(2,1)S(1)}, u32[]{:S(2)}, u32[]{:S(2)}) async-start(bf16[16,72,128]{2,1,0:T(8,128)(2,1)} %bitcast.5), calls=%async_computation | async-start | bytes 589824 | tf_op jit(solution)/shard_map/all_to_all | solution.py:548

commit v6 on v4

--- a/solution.py
+++ b/solution.py
@@ -508,11 +508,11 @@
     run(edges(newest + 1) + convolved(1), picks(newest + 3))
     run(edges(newest + 2) + convolved(2), activated(1))
     run(edges(newest + 3) + convolved(0) + convolved(3), activated(2))
+    run(mix(1) + mix(2))
     for k in range(4):
         wait_rows(k)
-    run(mix(1))
     run(product(1, 0) + product(1, 1), activated(0) + mix(0))
-    run(product(0, 0) + product(0, 1), mix(2))
+    run(product(0, 0) + product(0, 1))
     run(product(2, 0) + product(2, 1), activated(3) + mix(3))
     run(product(3, 0), finish(0, 0) + finish(0, 1))
     last = finish(1, 1)

time: 34.6 us -> 34.6 us (level)
  no operation moved by 1% of the time
where the time goes in v6:
time: 34.6 us; the launch traced here: 34.2 us
  Pallas kernels  25.3 us (73%)
  starting transfers between devices  7.43 us (21%)
  waiting for transfers between devices  1.42 us (4%)
    pallas_call x1, Pallas kernels, shards(): pl.pallas_call(functools.partial(main_kernel, devices, blocks, rows, half...  13.7 us
    pallas_call x1, Pallas kernels, shards(): pl.pallas_call(weight_kernel, grid=(3, 3), out_shape=jax.ShapeDtypeStruct...  9.12 us
    all_to_all x1, starting transfers between devices, shards(): lax.all_to_all(outgoing.reshape(chips, rows, 128), 'sp', split_axis=0, co...  7.43 us
    pallas_call x1, Pallas kernels, shards(): pl.pallas_call(functools.partial(pack_kernel, devices, rows, half, slots)...  2.51 us
    all_to_all x1, waiting for transfers between devices, shards(): lax.all_to_all(outgoing.reshape(chips, rows, 128), 'sp', split_axis=0, co...  1.42 us
  transfers between devices with their start and end apart: 1, of which 1 were waited for; matrix products, arithmetic and copies ran while one was open for 0% of the time, Pallas kernels for 27%

profile of v6, /device:TPU:0, one launch (start us, length us, event | category | flops | bytes accessed | tf_op | source)
XLA Modules:
  0.0 34.2 jit_solution(322440871702618882)
XLA Ops:
  0.0 0.0 copy-start.3
  0.0 0.0 copy-start.2
  0.0 0.0 copy-start.1
  0.0 0.0 copy-start
  0.0 2.5 %pack.1 = bf16[1152,128]{1,0:T(8,128)(2,1)} custom-call(s32[320]{0:T(512)} %cells_ref.1, bf16[64,320]{1,0:T(8,128)(2,1)} %bitcast.6), custom_call_target="tpu_custom_call" | custom-call | tf_op jit(solution)/shard_map/pack/pallas_call | solution.py:540
  2.5 7.4 %all-to-all-start = ((bf16[16,72,128]{2,1,0:T(8,128)(2,1)}), bf16[16,72,128]{2,1,0:T(8,128)(2,1)S(1)}, u32[]{:S(2)}, u32[]{:S(2)}) async-start(bf16[16,72,128]{2,1,0:T(8,128)(2,1)} %bitcast.5), calls=%async_computation | async-start | bytes 589824 | tf_op jit(solution)/shard_map/all_to_all | solution.py:547
  10.0 9.1 %weights.1.w_sum_hbm = bf16[2,3,3,384,384]{4,3,2,1,0:T(8,128)(2,1)} custom-call(bf16[3,3,3,384,384]{4,3,2,1,0:T(8,128)(2,1)} %w_mid_hbm.1), custom_call_target="tpu_custom_call" | custom-call | tf_op jit(solution)/shard_map/weights/pallas_call | solution.py:550
  19.1 1.4 %all-to-all-done = bf16[16,72,128]{2,1,0:T(8,128)(2,1)S(1)} async-done(((bf16[16,72,128]{2,1,0:T(8,128)(2,1)}), bf16[16,72,128]{2,1,0:T(8,128)(2,1)S(1)}, u32[]{:S(2)}, u32[]{:S(2)}) %all-to-all-start) | async-done | bytes 294944 | tf_op jit(solution)/shard_map/all_to_all | solution.py:547
  20.5 0.0 copy-done.3
  20.5 0.0 copy-done.2
  20.5 0.0 copy-done.1
  20.5 0.0 copy-done
  20.5 13.7 %block.1 = bf16[1280,384]{1,0:T(8,128)(2,1)} custom-call(bf16[1152,128]{1,0:T(8,128)(2,1)S(1)} %bitcast.4, bf16[3,3,3,16,384]{4,3,2,1,0:T(8,128)(2,1)S(1)} %copy-done, f32[384]{0:T(512)S(1)} %copy-done.1, f32[384]{0:T(512)S(1)} %copy-done.2, bf16[3,3,3,384,384]{4,3,2,1,0:T(8,128)(2,1)} %w_mid_hbm.1, bf16[2,3,3,384,384]{4,3,2,1,0:T(8,128)(2,1)} %weights.1.w_sum_hbm, ...), custom_call_target="tpu_custom_call" | custom-call | tf_op jit(solution)/shard_map/block/pallas_call | solution.py:561
Async XLA Ops:
  0.0 20.5 %copy-start.3 = (f32[384]{0:T(512)S(1)}, f32[384]{0:T(512)}, u32[]{:S(2)}) copy-start(f32[384]{0:T(512)} %b_mid_ref.1) | copy-start | bytes 4612
  0.0 20.5 %copy-start.2 = (f32[384]{0:T(512)S(1)}, f32[384]{0:T(512)}, u32[]{:S(2)}) copy-start(f32[384]{0:T(512)} %gain_ref.1) | copy-start | bytes 4612
  0.0 20.5 %copy-start.1 = (f32[384]{0:T(512)S(1)}, f32[384]{0:T(512)}, u32[]{:S(2)}) copy-start(f32[384]{0:T(512)} %b_in_ref.1) | copy-start | bytes 4612
  0.0 20.5 %copy-start = (bf16[3,3,3,16,384]{4,3,2,1,0:T(8,128)(2,1)S(1)}, bf16[3,3,3,16,384]{4,3,2,1,0:T(8,128)(2,1)}, u32[]{:S(2)}) copy-start(bf16[3,3,3,16,384]{4,3,2,1,0:T(8,128)(2,1)} %w_in_ref.1) | copy-start | bytes 995332
  2.5 18.0 %all-to-all-start = ((bf16[16,72,128]{2,1,0:T(8,128)(2,1)}), bf16[16,72,128]{2,1,0:T(8,128)(2,1)S(1)}, u32[]{:S(2)}, u32[]{:S(2)}) async-start(bf16[16,72,128]{2,1,0:T(8,128)(2,1)} %bitcast.5), calls=%async_computation | async-start | bytes 589824 | tf_op jit(solution)/shard_map/all_to_all | solution.py:547
